TPU v7x, 128 devices: a whole 4x4x4 slice. The times are simulated.
128 devices in a mesh: view: 2 (over z_lo), ty: 8 (over z_hi, y), tx: 8 (over x, core).
Axes of the slice: x: 4, y: 4, z: 4 (z_hi: 2, z_lo: 2; z = z_hi * 2 + z_lo), core: 2. Of those that a mesh axis runs over, the one named last changes fastest.
Arguments:
- views_data: float32 [2, 64, 256, 4096], P('view', None, 'ty', 'tx'), may hold values from 0.5 to 2
- psf_axial: float32 [2, 21], P('view'), may hold values from 0.2 to 1
- psf_rows: float32 [2, 7], P('view'), may hold values from 0.2 to 1
- psf_cols: float32 [2, 7], P('view'), may hold values from 0.2 to 1
Outputs:
- estimate: float32 [64, 256, 4096], P(None, 'ty', 'tx')
All inputs are finite; a program needn't handle non-finite values.
Results may differ from a plain program's by a relative error of at most 0.0001.
Values sent between devices are 32-bit elements; how exact they have to be, the bound alone decides.
No kernel may reach another device: no remote copies, remote signals or barrier semaphores. Data moves between devices by JAX's collectives and lax.ppermute only.
A program may use at most 128 MiB of HBM per device.

v0:
```python
import jax
import jax.numpy as jnp
from jax import lax
from jax.sharding import PartitionSpec as P

ITERS = 2


def from_partner(value, axis, stride):
    return lax.ppermute(value, axis, [(i, i ^ 1 << stride) for i in range(lax.axis_size(axis))])


def extended_2(block, sides, width):
    for axis, dim in sides:
        count = lax.axis_size(axis)
        forward = [(i, i + 1) for i in range(count - 1)]
        backward = [(target, source) for source, target in forward]
        low = lax.ppermute(
            lax.slice_in_dim(block, block.shape[dim] - width, None, axis=dim), axis, forward
        )
        high = lax.ppermute(lax.slice_in_dim(block, 0, width, axis=dim), axis, backward)
        block = jnp.concatenate([low, block, high], axis=dim)
    return block


def taps_pass(field, kernel, axis, length):
    running = kernel[0] * lax.slice_in_dim(field, 0, length, axis=axis)
    for offset in range(1, kernel.shape[0]):
        running = running + kernel[offset] * lax.slice_in_dim(
            field, offset, offset + length, axis=axis
        )
    return running


def padded_pass(field, kernel, axis):
    half_width = kernel.shape[0] // 2
    widths = [(0, 0), (0, 0), (0, 0)]
    widths[axis] = (half_width, half_width)
    return taps_pass(jnp.pad(field, widths), kernel, axis, field.shape[axis])


def per_device(views_data, psf_axial, psf_rows, psf_cols):
    recorded = views_data[0]
    kernel_z = psf_axial[0] / jnp.sum(psf_axial[0])
    kernel_y = psf_rows[0] / jnp.sum(psf_rows[0])
    kernel_x = psf_cols[0] / jnp.sum(psf_cols[0])
    tile_rows = recorded.shape[1]
    tile_cols = recorded.shape[2]
    radius = kernel_y.shape[0] // 2
    partner = from_partner(recorded, "view", 0)
    estimate = (recorded + partner) * 0.5
    for repeat in range(ITERS):
        extended = extended_2(estimate, (("ty", 1), ("tx", 2)), radius)
        blurred = padded_pass(extended, kernel_z, 0)
        blurred = taps_pass(blurred, kernel_y, 1, tile_rows)
        blurred = taps_pass(blurred, kernel_x, 2, tile_cols)
        ratio = recorded / blurred
        ratio_wide = extended_2(ratio, (("ty", 1), ("tx", 2)), radius)
        spread = taps_pass(ratio_wide, kernel_x[::-1], 2, tile_cols)
        spread = taps_pass(spread, kernel_y[::-1], 1, tile_rows)
        factor = padded_pass(spread, kernel_z[::-1], 0)
        other_factor = from_partner(factor, "view", 0)
        estimate = estimate * ((factor + other_factor) * 0.5)
    return estimate


def solution(mesh):
    placed = (P("view", None, "ty", "tx"), P("view", None), P("view", None), P("view", None))
    return jax.shard_map(
        per_device, mesh=mesh, in_specs=placed, out_specs=P(None, "ty", "tx"), check_vma=False
    )
```

profile of v0, /device:TPU:26, one launch (start us, length us, event | category | flops | bytes accessed | tf_op | source)
XLA Modules:
  0.0 958.0 jit_solution(2348001135790657259)
XLA Ops:
  0.0 6.7 copy.30
  11.9 87.5 %collective-permute-done = f32[64,32,512]{2,0,1:T(8,128)} collective-permute-done((f32[64,32,512]{2,0,1:T(8,128)}, f32[64,32,512]{2,0,1:T(8,128)}, u32[]{:S(2)}, u32[]{:S(2)}) %collective-permute-start) | collective-permute-done | bytes 4194336 | tf_op jit(solution)/shard_map/ppermute | solution.py:10
  99.5 6.4 add_multiply_fusion
  108.0 5.3 collective-permute-start.1
  120.7 7.7 collective-permute-done.2
  139.2 6.8 pad_maximum_fusion
  146.1 62.8 %fusion.20 = f32[64,38,518]{2,0,1:T(8,128)} fusion(f32[64,38,518]{2,0,1:T(8,128)} %pad_maximum_fusion, f32[]{:T(128)} %bitcast.29, f32[]{:T(128)} %bitcast.28, f32[]{:T(128)} %bitcast.27, f32[]{:T(128)} %bitcast.26, f32[]{:T(128)} %bitcast.25, f32[]{:T(128)} %bitcast.24, f32[]{:T(128)} %bitcast.23, f32[]{:T(128)} %bitcast.22, f32[]{:T(128)} %bitcast.21, ...), kind=kLoop, calls=%fused_computation.100 | loop fusion | flops 51650816 | bytes 10078292 | tf_op jit(solution)/shard_map/add | solution.py:29
  208.9 18.7 %fusion.86 = f32[64,32,518]{2,0,1:T(8,128)S(1)} fusion(f32[64,38,518]{2,0,1:T(8,128)} %fusion.20, f32[]{:T(128)} %bitcast.35, f32[]{:T(128)} %bitcast.34, f32[]{:T(128)} %bitcast.33, f32[]{:T(128)} %bitcast.32, f32[]{:T(128)} %bitcast.31, f32[]{:T(128)} %bitcast.30, f32[]{:T(128)} %bitcast.8), kind=kLoop, calls=%fused_computation.180 | loop fusion | flops 13791232 | bytes 33947676 | tf_op jit(solution)/shard_map/add | solution.py:29
  227.5 12.6 %fusion.204 = f32[64,32,512]{2,0,1:T(8,128)S(1)} fusion(f32[64,32,518]{2,0,1:T(8,128)S(1)} %fusion.86, f32[]{:T(128)} %bitcast.41, f32[]{:T(128)} %bitcast.40, f32[]{:T(128)} %bitcast.39, f32[]{:T(128)} %bitcast.38, f32[]{:T(128)} %bitcast.37, f32[]{:T(128)} %bitcast.36, f32[]{:T(128)} %bitcast.7, f32[1,64,32,512]{3,2,1,0:T(8,128)} %param.4), kind=kLoop, calls=%fused_computation.340 | loop fusion | flops 14680064 | bytes 37748764 | tf_op jit(solution)/shard_map/div | solution.py:57
  248.1 5.3 collective-permute-done.5
  253.5 5.5 collective-permute-done.6
  269.4 8.3 maximum_maximum_fusion
  277.7 20.4 %fusion.98 = f32[64,38,512]{2,0,1:T(8,128)S(1)} fusion(f32[64,38,515]{2,0,1:T(8,128)} %get-tuple-element.12, f32[64,38,515]{2,0,1:T(8,128)} %get-tuple-element.11, f32[]{:T(128)} %bitcast.47, f32[]{:T(128)} %bitcast.46, f32[]{:T(128)} %bitcast.45, f32[]{:T(128)} %bitcast.44, f32[]{:T(128)} %bitcast.43, f32[]{:T(128)} %bitcast.42, f32[]{:T(128)} %bitcast.6, ...), kind=kLoop, calls=%fused_computation.205 | loop fusion | flops 18677760 | bytes 39845916 | tf_op jit(solution)/shard_map/add | solution.py:29
  298.1 9.6 fusion.197
  307.7 62.8 %fusion.124 = f32[64,32,512]{2,0,1:T(8,128)S(1)} fusion(f32[64,32,512]{2,0,1:T(8,128)} %fusion.197, f32[]{:T(128)} %bitcast.73, f32[]{:T(128)} %bitcast.72, f32[]{:T(128)} %bitcast.71, f32[]{:T(128)} %bitcast.70, f32[]{:T(128)} %bitcast.69, f32[]{:T(128)} %bitcast.68, f32[]{:T(128)} %bitcast.67, f32[]{:T(128)} %bitcast.66, f32[]{:T(128)} %bitcast.65, ...), kind=kLoop, calls=%fused_computation.238 | loop fusion | flops 42991616 | bytes 8388692 | tf_op jit(solution)/shard_map/add | solution.py:29
  371.6 91.5 %collective-permute-done.9 = f32[64,32,512]{2,0,1:T(8,128)} collective-permute-done((f32[64,32,512]{2,0,1:T(8,128)S(1)}, f32[64,32,512]{2,0,1:T(8,128)}, u32[]{:S(2)}, u32[]{:S(2)}) %collective-permute-start.9) | collective-permute-done | bytes 4194336 | tf_op jit(solution)/shard_map/ppermute | solution.py:10
  463.1 66.5 %multiply_multiply_fusion.1 = f32[64,32,512]{2,0,1:T(8,128)} fusion(f32[64,32,512]{2,0,1:T(8,128)} %copy-done, f32[64,32,512]{2,0,1:T(8,128)} %collective-permute-done.9, f32[]{:T(128)} %bitcast.73, f32[]{:T(128)} %bitcast.72, f32[]{:T(128)} %bitcast.71, f32[]{:T(128)} %bitcast.70, f32[]{:T(128)} %bitcast.69, f32[]{:T(128)} %bitcast.68, f32[]{:T(128)} %bitcast.67, ...), kind=kLoop, calls=%fused_computation.354 | loop fusion | flops 46137344 | bytes 16777300 | tf_op jit(solution)/shard_map/mul | solution.py:63
  536.6 7.9 collective-permute-done.10
  544.5 5.5 collective-permute-done.11
  561.0 6.8 pad_maximum_fusion.2
  567.8 62.0 %fusion.60 = f32[64,38,518]{2,0,1:T(8,128)} fusion(f32[64,38,518]{2,0,1:T(8,128)} %pad_maximum_fusion.2, f32[]{:T(128)} %bitcast.29, f32[]{:T(128)} %bitcast.28, f32[]{:T(128)} %bitcast.27, f32[]{:T(128)} %bitcast.26, f32[]{:T(128)} %bitcast.25, f32[]{:T(128)} %bitcast.24, f32[]{:T(128)} %bitcast.23, f32[]{:T(128)} %bitcast.22, f32[]{:T(128)} %bitcast.21, ...), kind=kLoop, calls=%fused_computation.140 | loop fusion | flops 51650816 | bytes 10078292 | tf_op jit(solution)/shard_map/add | solution.py:29
  629.8 19.0 %fusion.80 = f32[64,32,518]{2,0,1:T(8,128)S(1)} fusion(f32[64,38,518]{2,0,1:T(8,128)} %fusion.60, f32[]{:T(128)} %bitcast.35, f32[]{:T(128)} %bitcast.34, f32[]{:T(128)} %bitcast.33, f32[]{:T(128)} %bitcast.32, f32[]{:T(128)} %bitcast.31, f32[]{:T(128)} %bitcast.30, f32[]{:T(128)} %bitcast.8), kind=kLoop, calls=%fused_computation.167 | loop fusion | flops 13791232 | bytes 33947676 | tf_op jit(solution)/shard_map/add | solution.py:29
  648.8 12.6 %fusion.191 = f32[64,32,512]{2,0,1:T(8,128)S(1)} fusion(f32[64,32,518]{2,0,1:T(8,128)S(1)} %fusion.80, f32[]{:T(128)} %bitcast.41, f32[]{:T(128)} %bitcast.40, f32[]{:T(128)} %bitcast.39, f32[]{:T(128)} %bitcast.38, f32[]{:T(128)} %bitcast.37, f32[]{:T(128)} %bitcast.36, f32[]{:T(128)} %bitcast.7, f32[1,64,32,512]{3,2,1,0:T(8,128)} %param.4), kind=kLoop, calls=%fused_computation.313 | loop fusion | flops 14680064 | bytes 37748764 | tf_op jit(solution)/shard_map/div | solution.py:57
  667.3 7.7 collective-permute-done.14
  675.0 5.5 collective-permute-done.15
  691.0 8.3 maximum_maximum_fusion.1
  699.3 20.4 %fusion.92 = f32[64,38,512]{2,0,1:T(8,128)S(1)} fusion(f32[64,38,515]{2,0,1:T(8,128)} %get-tuple-element.6, f32[64,38,515]{2,0,1:T(8,128)} %get-tuple-element.5, f32[]{:T(128)} %bitcast.47, f32[]{:T(128)} %bitcast.46, f32[]{:T(128)} %bitcast.45, f32[]{:T(128)} %bitcast.44, f32[]{:T(128)} %bitcast.43, f32[]{:T(128)} %bitcast.42, f32[]{:T(128)} %bitcast.6, ...), kind=kLoop, calls=%fused_computation.193 | loop fusion | flops 18677760 | bytes 39845916 | tf_op jit(solution)/shard_map/add | solution.py:29
  719.7 9.6 fusion.184
  729.3 62.4 %fusion.164 = f32[64,32,512]{2,0,1:T(8,128)S(1)} fusion(f32[64,32,512]{2,0,1:T(8,128)} %fusion.184, f32[]{:T(128)} %bitcast.73, f32[]{:T(128)} %bitcast.72, f32[]{:T(128)} %bitcast.71, f32[]{:T(128)} %bitcast.70, f32[]{:T(128)} %bitcast.69, f32[]{:T(128)} %bitcast.68, f32[]{:T(128)} %bitcast.67, f32[]{:T(128)} %bitcast.66, f32[]{:T(128)} %bitcast.65, ...), kind=kLoop, calls=%fused_computation.278 | loop fusion | flops 42991616 | bytes 8388692 | tf_op jit(solution)/shard_map/add | solution.py:29
  792.8 91.4 %collective-permute-done.18 = f32[64,32,512]{2,0,1:T(8,128)} collective-permute-done((f32[64,32,512]{2,0,1:T(8,128)S(1)}, f32[64,32,512]{2,0,1:T(8,128)}, u32[]{:S(2)}, u32[]{:S(2)}) %collective-permute-start.18) | collective-permute-done | bytes 4194336 | tf_op jit(solution)/shard_map/ppermute | solution.py:10
  884.2 66.8 %multiply_multiply_fusion = f32[64,32,512]{2,0,1:T(8,128)} fusion(f32[64,32,512]{2,0,1:T(8,128)} %multiply_multiply_fusion.1, f32[64,32,512]{2,0,1:T(8,128)} %collective-permute-done.18, f32[]{:T(128)} %bitcast.73, f32[]{:T(128)} %bitcast.72, f32[]{:T(128)} %bitcast.71, f32[]{:T(128)} %bitcast.70, f32[]{:T(128)} %bitcast.69, f32[]{:T(128)} %bitcast.68, ...), kind=kLoop, calls=%fused_computation.353 | loop fusion | flops 46137344 | bytes 16777300 | tf_op jit(solution)/shard_map/mul | solution.py:63
  951.0 6.6 copy.22
  (90 shorter events, 80.3 us)
Async XLA Ops:
  0.0 8.6 copy-start.7
  0.0 9.3 copy-start.8
  6.7 92.8 %collective-permute-start = (f32[64,32,512]{2,0,1:T(8,128)}, f32[64,32,512]{2,0,1:T(8,128)}, u32[]{:S(2)}, u32[]{:S(2)}) collective-permute-start(f32[64,32,512]{2,0,1:T(8,128)} %bitcast.84), channel_id=1, source_target_pairs={{0,64},{64,0},{1,65},{65,1},{2,66},{66,2},{3,67},{67,3},{4,68},{68... | collective-permute-start | bytes 12582920 | tf_op jit(solution)/shard_map/ppermute | solution.py:10
  11.9 103.9 %copy-start.9 = (f32[1,21]{1,0:T(1,128)S(1)}, f32[1,21]{1,0:T(1,128)}, u32[]{:S(2)}) copy-start(f32[1,21]{1,0:T(1,128)} %param.5) | copy-start | bytes 256
  105.9 2.0 copy-start
  108.0 12.8 %collective-permute-start.1 = (f32[64,3,512]{2,0,1:T(8,128)S(1)}, f32[64,3,512]{2,0,1:T(8,128)S(1)}, u32[]{:S(2)}, u32[]{:S(2)}) collective-permute-start(f32[64,3,512]{2,0,1:T(8,128)S(1)} %get-tuple-element.23), channel_id=1, source_target_pairs={{0,8},{8,16},{16,24},{24,32},{32,40},{40,48},{48,56},{1,9},{9,17},... | collective-permute-start | bytes 1179656 | tf_op jit(solution)/shard_map/ppermute | solution.py:18
  113.2 15.2 %collective-permute-start.2 = (f32[64,3,512]{2,0,1:T(8,128)S(1)}, f32[64,3,512]{2,0,1:T(8,128)S(1)}, u32[]{:S(2)}, u32[]{:S(2)}) collective-permute-start(f32[64,3,512]{2,0,1:T(8,128)S(1)} %get-tuple-element.24), channel_id=1, source_target_pairs={{8,0},{16,8},{24,16},{32,24},{40,32},{48,40},{56,48},{9,1},{17,9},... | collective-permute-start | bytes 1179656 | tf_op jit(solution)/shard_map/ppermute | solution.py:21
  130.9 6.8 collective-permute-start.3
  133.3 5.5 collective-permute-start.4
  240.1 19.8 %copy-start.1 = (f32[64,32,512]{2,0,1:T(8,128)}, f32[64,32,512]{2,0,1:T(8,128)S(1)}, u32[]{:S(2)}) copy-start(f32[64,32,512]{2,0,1:T(8,128)S(1)} %fusion.204) | copy-start | bytes 12582916
  240.2 13.3 %collective-permute-start.5 = (f32[64,3,512]{2,0,1:T(8,128)S(1)}, f32[64,3,512]{2,0,1:T(8,128)S(1)}, u32[]{:S(2)}, u32[]{:S(2)}) collective-permute-start(f32[64,3,512]{2,0,1:T(8,128)S(1)} %get-tuple-element.21), channel_id=1, source_target_pairs={{0,8},{8,16},{16,24},{24,32},{32,40},{40,48},{48,56},{1,9},{9,17},... | collective-permute-start | bytes 1179656 | tf_op jit(solution)/shard_map/ppermute | solution.py:18
  242.1 16.9 %collective-permute-start.6 = (f32[64,3,512]{2,0,1:T(8,128)S(1)}, f32[64,3,512]{2,0,1:T(8,128)S(1)}, u32[]{:S(2)}, u32[]{:S(2)}) collective-permute-start(f32[64,3,512]{2,0,1:T(8,128)S(1)} %get-tuple-element.22), channel_id=1, source_target_pairs={{8,0},{16,8},{24,16},{32,24},{40,32},{48,40},{56,48},{9,1},{17,9},... | collective-permute-start | bytes 1179656 | tf_op jit(solution)/shard_map/ppermute | solution.py:21
  253.5 16.0 %copy-start.3 = (f32[64,3,512]{2,0,1:T(8,128)}, f32[64,3,512]{2,0,1:T(8,128)S(1)}, u32[]{:S(2)}) copy-start(f32[64,3,512]{2,0,1:T(8,128)S(1)} %collective-permute-done.5) | copy-start | bytes 1179652
  259.0 10.4 %copy-start.4 = (f32[64,3,512]{2,0,1:T(8,128)}, f32[64,3,512]{2,0,1:T(8,128)S(1)}, u32[]{:S(2)}) copy-start(f32[64,3,512]{2,0,1:T(8,128)S(1)} %collective-permute-done.6) | copy-start | bytes 1179652
  260.9 6.9 collective-permute-start.7
  263.9 5.1 collective-permute-start.8
  370.5 92.6 %collective-permute-start.9 = (f32[64,32,512]{2,0,1:T(8,128)S(1)}, f32[64,32,512]{2,0,1:T(8,128)}, u32[]{:S(2)}, u32[]{:S(2)}) collective-permute-start(f32[64,32,512]{2,0,1:T(8,128)S(1)} %fusion.124), channel_id=1, source_target_pairs={{0,64},{64,0},{1,65},{65,1},{2,66},{66,2},{3,67},{67,3},{4,68},{68... | collective-permute-start | bytes 12582920 | tf_op jit(solution)/shard_map/ppermute | solution.py:10
  530.8 13.7 %collective-permute-start.10 = (f32[64,3,512]{2,0,1:T(8,128)S(1)}, f32[64,3,512]{2,0,1:T(8,128)S(1)}, u32[]{:S(2)}, u32[]{:S(2)}) collective-permute-start(f32[64,3,512]{2,0,1:T(8,128)S(1)} %get-tuple-element.19), channel_id=1, source_target_pairs={{0,8},{8,16},{16,24},{24,32},{32,40},{40,48},{48,56},{1,9},{9,17},... | collective-permute-start | bytes 1179656 | tf_op jit(solution)/shard_map/ppermute | solution.py:18
  532.7 17.4 %collective-permute-start.11 = (f32[64,3,512]{2,0,1:T(8,128)S(1)}, f32[64,3,512]{2,0,1:T(8,128)S(1)}, u32[]{:S(2)}, u32[]{:S(2)}) collective-permute-start(f32[64,3,512]{2,0,1:T(8,128)S(1)} %get-tuple-element.20), channel_id=1, source_target_pairs={{8,0},{16,8},{24,16},{32,24},{40,32},{48,40},{56,48},{9,1},{17,9},... | collective-permute-start | bytes 1179656 | tf_op jit(solution)/shard_map/ppermute | solution.py:21
  552.5 6.2 collective-permute-start.12
  555.1 5.5 collective-permute-start.13
  661.4 20.1 %copy-start.2 = (f32[64,32,512]{2,0,1:T(8,128)}, f32[64,32,512]{2,0,1:T(8,128)S(1)}, u32[]{:S(2)}) copy-start(f32[64,32,512]{2,0,1:T(8,128)S(1)} %fusion.191) | copy-start | bytes 12582916
  661.4 13.6 %collective-permute-start.14 = (f32[64,3,512]{2,0,1:T(8,128)S(1)}, f32[64,3,512]{2,0,1:T(8,128)S(1)}, u32[]{:S(2)}, u32[]{:S(2)}) collective-permute-start(f32[64,3,512]{2,0,1:T(8,128)S(1)} %get-tuple-element.17), channel_id=1, source_target_pairs={{0,8},{8,16},{16,24},{24,32},{32,40},{40,48},{48,56},{1,9},{9,17},... | collective-permute-start | bytes 1179656 | tf_op jit(solution)/shard_map/ppermute | solution.py:18
  663.4 17.2 %collective-permute-start.15 = (f32[64,3,512]{2,0,1:T(8,128)S(1)}, f32[64,3,512]{2,0,1:T(8,128)S(1)}, u32[]{:S(2)}, u32[]{:S(2)}) collective-permute-start(f32[64,3,512]{2,0,1:T(8,128)S(1)} %get-tuple-element.18), channel_id=1, source_target_pairs={{8,0},{16,8},{24,16},{32,24},{40,32},{48,40},{56,48},{9,1},{17,9},... | collective-permute-start | bytes 1179656 | tf_op jit(solution)/shard_map/ppermute | solution.py:21
  675.0 16.0 %copy-start.5 = (f32[64,3,512]{2,0,1:T(8,128)}, f32[64,3,512]{2,0,1:T(8,128)S(1)}, u32[]{:S(2)}) copy-start(f32[64,3,512]{2,0,1:T(8,128)S(1)} %collective-permute-done.14) | copy-start | bytes 1179652
  680.6 10.4 %copy-start.6 = (f32[64,3,512]{2,0,1:T(8,128)}, f32[64,3,512]{2,0,1:T(8,128)S(1)}, u32[]{:S(2)}) copy-start(f32[64,3,512]{2,0,1:T(8,128)S(1)} %collective-permute-done.15) | copy-start | bytes 1179652
  682.4 6.3 collective-permute-start.16
  685.0 5.5 collective-permute-start.17
  791.7 92.5 %collective-permute-start.18 = (f32[64,32,512]{2,0,1:T(8,128)S(1)}, f32[64,32,512]{2,0,1:T(8,128)}, u32[]{:S(2)}, u32[]{:S(2)}) collective-permute-start(f32[64,32,512]{2,0,1:T(8,128)S(1)} %fusion.164), channel_id=1, source_target_pairs={{0,64},{64,0},{1,65},{65,1},{2,66},{66,2},{3,67},{67,3},{4,68},{68... | collective-permute-start | bytes 12582920 | tf_op jit(solution)/shard_map/ppermute | solution.py:10
where the time goes:
time: 966 us; the launch traced here: 958 us
  other arithmetic  552 us (57%)
  waiting for transfers between devices  323 us (33%)
  starting transfers between devices  51.9 us (5%)
  local copies, waits for them, and re-layouts  30.6 us (3%)
    add x10, other arithmetic, taps_pass(): running + kernel[offset] * lax.slice_in_dim(field, offset, offset + lengt...  348 us
    ppermute x3, waiting for transfers between devices, from_partner(): lax.ppermute(value, axis, [(i, i ^ 1 << stride) for i in range(lax.axis_s...  270 us
    mul x2, other arithmetic, per_device(): estimate = estimate * ((factor + other_factor) * 0.5)  133 us
    concatenate x6, other arithmetic, extended_2(): block = jnp.concatenate([low, block, high], axis=dim)  32 us
    ppermute x8, waiting for transfers between devices, extended_2(): lax.ppermute(lax.slice_in_dim(block, 0, width, axis=dim), axis, backward)  28.4 us
    ppermute x8, starting transfers between devices, extended_2(): lax.ppermute(lax.slice_in_dim(block, 0, width, axis=dim), axis, backward)  28 us
    div x2, other arithmetic, per_device(): ratio = recorded / blurred  25.1 us
    ppermute x8, waiting for transfers between devices, extended_2(): lax.ppermute(lax.slice_in_dim(block, block.shape[dim] - width, None, axis...  23.7 us
  transfers between devices with their start and end apart: 19, of which 15 were waited for; matrix products, arithmetic and copies ran while one was open for 1% of the time, Pallas kernels for 0%

commit v1 on v0

v1 whole, which is shorter than its diff:
```python
import functools

import jax
import jax.numpy as jnp
from jax import lax
from jax.experimental import pallas as pl
from jax.experimental.pallas import tpu as pltpu
from jax.sharding import PartitionSpec as P

ITERS = 2
Z = 64
LANES = 128
ROWS = 32
HALF = 256
CHUNK = 128
PAD = 6
SIDE = 8
EXT_R = ROWS + 2 * PAD
EXT_C = HALF + 2 * SIDE
VMEM_BYTES = 48 * 1024 * 1024
TINY = 1e-30


def params(**kwargs):
    return pltpu.CompilerParams(vmem_limit_bytes=VMEM_BYTES, **kwargs)


def blocks_of(total, largest=96):
    out, at = [], 0
    while at < total:
        size = min(largest, total - at)
        out.append((at, size))
        at += size
    return out


def matrices_kernel(kz_ref, blur_ref, adj_ref):
    taps = kz_ref.shape[0]
    lane = lax.broadcasted_iota(jnp.int32, (Z, LANES), 1)
    row = lax.broadcasted_iota(jnp.int32, (Z, LANES), 0)
    offset = row - lax.rem(lane, Z) + taps // 2
    mat = jnp.zeros((Z, LANES), jnp.float32)
    for t in range(taps):
        mat = mat + jnp.where(offset == t, kz_ref[t : t + 1, :], 0.0)
    high = mat.astype(jnp.bfloat16)
    low = (mat - high.astype(jnp.float32)).astype(jnp.bfloat16)
    blur_ref[0:Z, 0:LANES] = high
    blur_ref[0:Z, LANES:] = low
    blur_ref[Z:, 0:LANES] = high
    blur_ref[Z:, LANES:] = jnp.zeros((Z, LANES), jnp.bfloat16)
    adj = jnp.concatenate([mat, mat], axis=0).T * 0.5
    ahigh = adj.astype(jnp.bfloat16).astype(jnp.float32)
    alow = adj - ahigh
    first = lax.broadcasted_iota(jnp.int32, (LANES, LANES), 1) < Z
    adj_ref[0:LANES, :] = jnp.where(first, ahigh, alow).astype(jnp.bfloat16)
    adj_ref[LANES:, :] = jnp.where(first, ahigh, 0.0).astype(jnp.bfloat16)


def matrices(kz):
    return pl.pallas_call(
        matrices_kernel,
        out_shape=(
            jax.ShapeDtypeStruct((2 * Z, 2 * LANES), jnp.bfloat16),
            jax.ShapeDtypeStruct((2 * LANES, LANES), jnp.bfloat16),
        ),
        compiler_params=params(),
        name="matrices",
    )(kz)


def turn_kernel(where_ref, own_ref, other_ref, out_ref):
    rows = own_ref.shape[2]
    own = own_ref.reshape(Z * rows, CHUNK)
    other = other_ref.reshape(Z * rows, CHUNK)
    first = where_ref[1] == 0
    for y in range(rows):
        mine = own[pl.ds(y, Z, stride=rows), :]
        theirs = other[pl.ds(y, Z, stride=rows), :]
        pair = jnp.concatenate(
            [jnp.where(first, mine, theirs), jnp.where(first, theirs, mine)], axis=0
        )
        out_ref[y] = pair.T


def turn(where, recorded, received):
    rows = 8
    return pl.pallas_call(
        turn_kernel,
        out_shape=jax.ShapeDtypeStruct((ROWS, CHUNK, LANES), jnp.float32),
        grid_spec=pltpu.PrefetchScalarGridSpec(
            num_scalar_prefetch=1,
            grid=(ROWS // rows,),
            in_specs=[
                pl.BlockSpec((1, Z, rows, CHUNK), lambda i, w: (0, 0, i, w[0])),
                pl.BlockSpec((Z, rows, CHUNK), lambda i, w: (0, i, 0)),
            ],
            out_specs=pl.BlockSpec((rows, CHUNK, LANES), lambda i, w: (i, 0, 0)),
        ),
        cost_estimate=pl.CostEstimate(flops=0, bytes_accessed=4 << 20, transcendentals=0),
        compiler_params=params(),
        name="turn",
    )(where, recorded, received)


def iterate_kernel(first, start, width, final, *refs):
    if first:
        field = None
        recorded, refs = refs[:5], refs[5:]
    else:
        field, recorded, refs = refs[:5], refs[5:10], refs[10:]
    taps_ref, blur_ref, adj_ref, out_ref = refs[:4]
    r_buf, e_buf, xz_buf, xr_buf, tmp, r_sem, e_sem = refs[4:]

    groups = [(0, PAD)] + [(PAD + 8 * i, 8) for i in range(ROWS // 8)] + [(EXT_R - PAD, PAD)]

    def copies(pieces, buf, sems, group):
        top, left, mid, right, bottom = pieces
        row, count = groups[group]
        stop = start + width
        out = []
        if group == 0 or group == len(groups) - 1:
            src = top if group == 0 else bottom
            out.append((src.at[:, pl.ds(start, width), :], buf.at[pl.ds(row, count), :, :]))
        else:
            for src, lo, hi in (
                (left, 0, SIDE),
                (mid, SIDE, SIDE + HALF),
                (right, SIDE + HALF, EXT_C),
            ):
                a, b = max(lo, start), min(hi, stop)
                if a < b:
                    out.append(
                        (
                            src.at[pl.ds(row - PAD, count), pl.ds(a - lo, b - a), :],
                            buf.at[pl.ds(row, count), pl.ds(a - start, b - a), :],
                        )
                    )
        return [
            pltpu.make_async_copy(src, dst, sems.at[group, k])
            for k, (src, dst) in enumerate(out)
        ]

    r_copies = [copies(recorded, r_buf, r_sem, g) for g in range(len(groups))]
    e_copies = [[] for _ in groups] if first else [copies(field, e_buf, e_sem, g) for g in range(len(groups))]
    if first:
        for g in range(len(groups)):
            for c in r_copies[g]:
                c.start()
    else:
        for g in range(len(groups)):
            for c in e_copies[g]:
                c.start()
        for g in range(len(groups)):
            for c in r_copies[g]:
                c.start()

    kx = [taps_ref[t : t + 1, :] for t in range(7)]
    ky = [taps_ref[8 + t : 9 + t, :] for t in range(7)]
    col_blocks = blocks_of(width)
    lower = lax.broadcasted_iota(jnp.int32, (width, LANES), 1) < Z

    def cols_pass(slot, taps, dst_ref, row):
        for at, size in col_blocks:
            acc = taps[0] * tmp[slot, pl.ds(5 + at, size), :]
            for t in range(1, 7):
                acc = acc + taps[t] * tmp[slot, pl.ds(5 + t + at, size), :]
            dst_ref[row, pl.ds(at, size), :] = acc

    def blur_row(slot, row):
        if first:
            r = r_buf[row]
            e = (r + pltpu.roll(r, Z, 1)) * 0.5
            e_buf[row] = e
        else:
            e = e_buf[row]
        high = e.astype(jnp.bfloat16).astype(jnp.float32)
        split = jnp.where(lower, high, e - high).astype(jnp.bfloat16)
        both = jnp.dot(split, blur_ref[...], preferred_element_type=jnp.float32)
        tmp[slot, pl.ds(8, width), :] = both[:, :LANES] + both[:, LANES:]
        cols_pass(slot, kx, xz_buf, row)

    for slot in range(2):
        tmp[slot, pl.ds(0, 8), :] = jnp.zeros((8, LANES), jnp.float32)
        tmp[slot, pl.ds(8 + width, 8), :] = jnp.zeros((8, LANES), jnp.float32)

    for g, (row0, count) in enumerate(groups):
        for c in r_copies[g] if first else e_copies[g]:
            c.wait()

        def body(i, carry, row0=row0):
            blur_row(0, row0 + 2 * i)
            blur_row(1, row0 + 2 * i + 1)
            return carry

        lax.fori_loop(0, count // 2, body, 0)

    if not first:
        for g in range(len(groups)):
            for c in r_copies[g]:
                c.wait()

    def rows_pass(src_ref, taps, row, at, size):
        acc = taps[0] * src_ref[row - 3, pl.ds(at, size), :]
        for t in range(1, 7):
            acc = acc + taps[t] * src_ref[row - 3 + t, pl.ds(at, size), :]
        return acc

    def ratio_row(slot, row):
        for at, size in col_blocks:
            blurred = rows_pass(xz_buf, ky, row, at, size)
            ratio = r_buf[row, pl.ds(at, size), :] / jnp.maximum(blurred, TINY)
            tmp[slot, pl.ds(8 + at, size), :] = ratio
        cols_pass(slot, kx[::-1], xr_buf, row)

    def ratio_body(i, carry):
        ratio_row(0, 3 + 2 * i)
        ratio_row(1, 4 + 2 * i)
        return carry

    lax.fori_loop(0, (EXT_R - 6) // 2, ratio_body, 0)

    inner = width - 2 * SIDE

    def update_row(row):
        spread = []
        for at, size in blocks_of(inner, 64):
            spread.append(rows_pass(xr_buf, ky[::-1], row, SIDE + at, size))
        spread = jnp.concatenate(spread, axis=0)
        high = spread.astype(jnp.bfloat16)
        low = (spread - high.astype(jnp.float32)).astype(jnp.bfloat16)
        both = jnp.dot(
            jnp.concatenate([high, low], axis=1), adj_ref[...], preferred_element_type=jnp.float32
        )
        factor = both + pltpu.roll(both, Z, 1)
        return e_buf[row, pl.ds(SIDE, inner), :] * factor

    if final:
        flat = out_ref.reshape(Z * ROWS, CHUNK)

    def update_body(i, carry):
        for k in range(2):
            y = 2 * i + k
            new = update_row(PAD + y)
            if final:
                flat[pl.ds(y, Z, stride=ROWS), :] = new.T[:Z]
            else:
                out_ref[y] = new
        return carry

    lax.fori_loop(0, ROWS // 2, update_body, 0)


def iterate(field, recorded, taps, blur, adj, *, first, start, width, final):
    inner = width - 2 * SIDE
    out = (Z, ROWS, inner) if final else (ROWS, inner, LANES)
    pieces = list(recorded) if first else list(field) + list(recorded)
    row = pltpu.VMEM((EXT_R, width, LANES), jnp.float32)
    vregs = EXT_R * width // 8
    return pl.pallas_call(
        functools.partial(iterate_kernel, first, start, width, final),
        out_shape=jax.ShapeDtypeStruct(out, jnp.float32),
        in_specs=[pl.BlockSpec(memory_space=pl.ANY)] * len(pieces)
        + [pl.BlockSpec(memory_space=pltpu.VMEM)] * 3,
        out_specs=pl.BlockSpec(memory_space=pltpu.VMEM),
        scratch_shapes=[
            row,
            row,
            row,
            row,
            pltpu.VMEM((2, width + 16, LANES), jnp.float32),
            pltpu.SemaphoreType.DMA((6, 3)),
            pltpu.SemaphoreType.DMA((6, 3)),
        ],
        cost_estimate=pl.CostEstimate(
            flops=vregs * 1024 * 70, bytes_accessed=vregs * 4096 * 3, transcendentals=0
        ),
        compiler_params=params(),
        name="iterate",
    )(*pieces, taps, blur, adj)


def place_kernel(where_ref, *refs):
    refs[-1][...] = refs[0][...]


def place(where, block, whole):
    rows = 16
    spec = pl.BlockSpec((rows, ROWS, CHUNK), lambda i, w: (i, 0, 0))
    args = [where, block]
    in_specs = [spec]
    aliases = {}
    if whole is not None:
        args.append(whole)
        in_specs.append(pl.BlockSpec(memory_space=pl.ANY))
        aliases = {2: 0}
    return pl.pallas_call(
        place_kernel,
        out_shape=jax.ShapeDtypeStruct((Z, ROWS, 2 * HALF), jnp.float32),
        grid_spec=pltpu.PrefetchScalarGridSpec(
            num_scalar_prefetch=1,
            grid=(Z // rows,),
            in_specs=in_specs,
            out_specs=pl.BlockSpec((rows, ROWS, CHUNK), lambda i, w: (i, 0, w[0])),
        ),
        input_output_aliases=aliases,
        cost_estimate=pl.CostEstimate(flops=0, bytes_accessed=2 << 20, transcendentals=0),
        compiler_params=params(),
        name="place",
    )(*args)


def neighbours(views, tiles):
    right = []
    for v in range(views):
        for t in range(tiles):
            if (t + v) % 2 == 0:
                right.append((v * tiles + t, (1 - v) * tiles + t))
            elif t + 1 < tiles:
                right.append((v * tiles + t, v * tiles + t + 1))
    return right


def per_device(views_data, psf_axial, psf_rows, psf_cols):
    views, tiles, bands = lax.axis_size("view"), lax.axis_size("tx"), lax.axis_size("ty")
    swap = [(0, 1), (1, 0)]
    right = neighbours(views, tiles)
    left = [(b, a) for a, b in right]
    down = [(i, i + 1) for i in range(bands - 1)]
    up = [(b, a) for a, b in down]
    half = lax.rem(lax.axis_index("tx") + lax.axis_index("view"), 2)

    def other_block(j):
        at = (1 - half) * HALF + j * CHUNK
        return lax.dynamic_slice(views_data, (0, 0, 0, at), (1, Z, ROWS, CHUNK))[0]

    incoming = [lax.ppermute(other_block(j), "view", swap) for j in range(2)]

    norm = lambda k: k[0] / jnp.sum(k[0])
    own = jnp.concatenate([norm(psf_axial), norm(psf_rows), norm(psf_cols)])
    other = lax.ppermute(own, "view", swap)
    view = lax.axis_index("view")
    lanes = jnp.concatenate(
        [
            jnp.broadcast_to(jnp.where(view == 0, own, other)[:, None], (own.shape[0], Z)),
            jnp.broadcast_to(jnp.where(view == 0, other, own)[:, None], (own.shape[0], Z)),
        ],
        axis=1,
    )
    blur, adj = matrices(lanes[:21])
    taps = jnp.zeros((16, LANES), jnp.float32)
    taps = taps.at[0:7].set(lanes[28:35]).at[8:15].set(lanes[21:28])

    mid = jnp.concatenate(
        [
            turn(jnp.stack([half * 2 + j, view]).astype(jnp.int32), views_data, incoming[j])
            for j in range(2)
        ],
        axis=1,
    )

    def extend(block):
        west = lax.ppermute(block[:, HALF - SIDE :], ("view", "tx"), right)
        east = lax.ppermute(block[:, :SIDE], ("view", "tx"), left)

        def edge(rows):
            return jnp.concatenate([west[rows], block[rows], east[rows]], axis=1)

        north = lax.ppermute(edge(slice(ROWS - PAD, ROWS)), "ty", down)
        south = lax.ppermute(edge(slice(0, PAD)), "ty", up)
        return north, west, block, east, south

    recorded = extend(mid)
    estimate = iterate(
        None, recorded, taps, blur, adj, first=True, start=0, width=EXT_C, final=False
    )
    field = extend(estimate)
    outs = [
        iterate(
            field,
            recorded,
            taps,
            blur,
            adj,
            first=False,
            start=j * CHUNK,
            width=CHUNK + 2 * SIDE,
            final=True,
        )
        for j in range(2)
    ]
    theirs = [lax.ppermute(o, "view", swap) for o in outs]
    whole = None
    for j, block in enumerate(outs):
        whole = place((half * 2 + j).astype(jnp.int32)[None], block, whole)
    for j, block in enumerate(theirs):
        whole = place(((1 - half) * 2 + j).astype(jnp.int32)[None], block, whole)
    return whole


def solution(mesh):
    placed = (P("view", None, "ty", "tx"), P("view", None), P("view", None), P("view", None))
    return jax.shard_map(
        per_device, mesh=mesh, in_specs=placed, out_specs=P(None, "ty", "tx"), check_vma=False
    )
```

time: 966 us -> 220 us (0.23)
  other arithmetic: 552 us -> 10.5 us
  waiting for transfers between devices: 323 us -> 110 us
  Pallas kernels: 0 us -> 64.3 us
  local copies, waits for them, and re-layouts: 30.6 us -> 5.47 us
  starting transfers between devices: 51.9 us -> 28.8 us
    add x10 -> x0, other arithmetic: 348 us -> none  [taps_pass(): running + kernel[offset] * lax.slice_in_dim(field, offset, offset + lengt...]
    ppermute x19 -> x13, waiting for transfers between devices: 323 us -> 110 us  [the longest x2 35.5 us: per_device(): incoming = [lax.ppermute(other_block(j), 'view', swap) for j in range(2)]]
    mul x3 -> x0, other arithmetic: 140 us -> none  [the longest x2 133 us: per_device(): estimate = estimate * ((factor + other_factor) * 0.5)]
    pallas_call x0 -> x10, Pallas kernels: none -> 64.3 us  [the longest x3 49.7 us: iterate(): pl.pallas_call(functools.partial(iterate_kernel, first, start, width, fin...]
    concatenate x6 -> x8, other arithmetic: 32 us -> 6.27 us  [the longest x2 4.08 us: per_device(): jnp.concatenate([turn(jnp.stack([half * 2 + j, view]).astype(jnp.int32),...]
    div x5 -> x2, other arithmetic: 27 us -> 1.95 us  [per_device(): norm = lambda k: k[0] / jnp.sum(k[0])]
    ppermute x19 -> x13, starting transfers between devices: 51.9 us -> 28.8 us  [the longest x2 7.37 us: extend(): north = lax.ppermute(edge(slice(ROWS - PAD, ROWS)), 'ty', down)]
  transfers between devices with their start and end apart: 19 -> 13, of which waited for: 15 -> 11; matrix products, arithmetic and copies ran while one was open for 1% -> 5% of each run, Pallas kernels for 0% -> 12%
where the time goes in v1:
time: 220 us; the launch traced here: 219 us
  waiting for transfers between devices  110 us (50%)
  Pallas kernels  64.3 us (29%)
  starting transfers between devices  28.8 us (13%)
  other arithmetic  10.5 us (5%)
  local copies, waits for them, and re-layouts  5.47 us (2%)
    pallas_call x3, Pallas kernels, iterate(): pl.pallas_call(functools.partial(iterate_kernel, first, start, width, fin...  49.7 us
    ppermute x2, waiting for transfers between devices, per_device(): incoming = [lax.ppermute(other_block(j), 'view', swap) for j in range(2)]  35.5 us
    ppermute x2, waiting for transfers between devices, per_device(): theirs = [lax.ppermute(o, 'view', swap) for o in outs]  24.6 us
    ppermute x2, waiting for transfers between devices, extend(): north = lax.ppermute(edge(slice(ROWS - PAD, ROWS)), 'ty', down)  23.9 us
    ppermute x2, waiting for transfers between devices, extend(): south = lax.ppermute(edge(slice(0, PAD)), 'ty', up)  14.3 us
    ppermute x2, waiting for transfers between devices, extend(): east = lax.ppermute(block[:, :SIDE], ('view', 'tx'), left)  7.98 us
    pallas_call x4, Pallas kernels, place(): pl.pallas_call(place_kernel, out_shape=jax.ShapeDtypeStruct((Z, ROWS, 2 *...  7.93 us
    ppermute x2, starting transfers between devices, extend(): north = lax.ppermute(edge(slice(ROWS - PAD, ROWS)), 'ty', down)  7.37 us
  transfers between devices with their start and end apart: 13, of which 11 were waited for; matrix products, arithmetic and copies ran while one was open for 5% of the time, Pallas kernels for 12%

profile of v1, /device:TPU:26, one launch (start us, length us, event | category | flops | bytes accessed | tf_op | source)
XLA Modules:
  0.0 219.1 jit_solution(11344724367735972487)
XLA Ops:
  0.0 2.7 %dynamic-slice_bitcast_fusion.1 = (f32[64,32,128]{2,1,0:T(8,128)S(1)}, f32[64,32,128]{2,1,0:T(8,128)}) fusion(f32[1,64,32,512]{3,2,1,0:T(8,128)} %own_ref.3, s32[]{:T(128)S(6)} %select_n.18, s32[]{:T(128)S(6)} %select_n.19), kind=kLoop, calls=%fused_computation.6 | loop fusion | bytes 4194312 | tf_op jit(solution)/shard_map/squeeze | solution.py:334
  2.7 1.9 collective-permute-start
  8.8 20.0 %collective-permute-done.other_ref = f32[64,32,128]{2,1,0:T(8,128)S(1)} collective-permute-done((f32[64,32,128]{2,1,0:T(8,128)S(1)}, f32[64,32,128]{2,1,0:T(8,128)S(1)}, u32[]{:S(2)}, u32[]{:S(2)}) %collective-permute-start) | collective-permute-done | bytes 1048608 | tf_op jit(solution)/shard_map/ppermute | solution.py:336
  28.8 3.2 %turn.2 = f32[32,128,128]{2,1,0:T(8,128)S(1)} custom-call(s32[2]{0:T(128)S(1)} %get-tuple-element.51.where_ref, f32[1,64,32,512]{3,2,1,0:T(8,128)} %own_ref.3, f32[64,32,128]{2,1,0:T(8,128)S(1)} %collective-permute-done.other_ref), custom_call_target="tpu_custom_call" | custom-call | bytes 4194304 | tf_op jit(solution)/shard_map/turn/pallas_call | solution.py:87
  32.0 3.8 %collective-permute-start.1 = (f32[32,8,128]{2,1,0:T(8,128)S(1)}, f32[32,8,128]{2,1,0:T(8,128)S(1)}, u32[]{:S(2)}, u32[]{:S(2)}) collective-permute-start(f32[32,8,128]{2,1,0:T(8,128)S(1)} %slice.109), channel_id=1, source_target_pairs={{0,64},{1,2},{2,66},{3,4},{4,68},{5,6},{6,70},{64,65},{65,1},{66,6... | collective-permute-start | bytes 393224 | tf_op jit(solution)/shard_map/ppermute | solution.py:362
  35.8 15.5 %collective-permute-done.2.other_ref = f32[64,32,128]{2,1,0:T(8,128)} collective-permute-done((f32[64,32,128]{2,1,0:T(8,128)}, f32[64,32,128]{2,1,0:T(8,128)}, u32[]{:S(2)}, u32[]{:S(2)}) %collective-permute-start.2) | collective-permute-done | bytes 1048608 | tf_op jit(solution)/shard_map/ppermute | solution.py:336
  51.3 3.3 %turn.3 = f32[32,128,128]{2,1,0:T(8,128)S(1)} custom-call(s32[2]{0:T(128)S(1)} %get-tuple-element.52.where_ref, f32[1,64,32,512]{3,2,1,0:T(8,128)} %own_ref.3, f32[64,32,128]{2,1,0:T(8,128)} %collective-permute-done.2.other_ref), custom_call_target="tpu_custom_call" | custom-call | bytes 4194304 | tf_op jit(solution)/shard_map/turn/pallas_call | solution.py:87
  54.7 1.9 collective-permute-start.3
  56.8 4.8 %collective-permute-done.3.refs_3_.refs_8_ = f32[32,8,128]{2,1,0:T(8,128)S(1)} collective-permute-done((f32[32,8,128]{2,1,0:T(8,128)S(1)}, f32[32,8,128]{2,1,0:T(8,128)S(1)}, u32[]{:S(2)}, u32[]{:S(2)}) %collective-permute-start.3) | collective-permute-done | bytes 131104 | tf_op jit(solution)/shard_map/ppermute | solution.py:363
  62.5 5.4 %collective-permute-start.4 = (f32[6,272,128]{2,1,0:T(8,128)}, f32[6,272,128]{2,1,0:T(8,128)S(1)}, u32[]{:S(2)}, u32[]{:S(2)}) collective-permute-start(f32[6,272,128]{2,1,0:T(8,128)} %pad_maximum_fusion.1), channel_id=1, source_target_pairs={{0,8},{8,16},{16,24},{24,32},{32,40},{40,48},{48,56},{1,9},{9,17},... | collective-permute-start | bytes 2506760 | tf_op jit(solution)/shard_map/ppermute | solution.py:368
  68.9 1.9 collective-permute-start.5
  71.0 3.5 %collective-permute-done.6 = f32[35]{0:T(128)S(1)} collective-permute-done((f32[35]{0:T(128)S(1)}, f32[35]{0:T(128)S(1)}, u32[]{:S(2)}, u32[]{:S(2)}) %collective-permute-start.6) | collective-permute-done | bytes 172 | tf_op jit(solution)/shard_map/ppermute | solution.py:340
  75.2 4.0 %pad_maximum_fusion.refs_2_.refs_7_ = f32[32,256,128]{2,1,0:T(8,128)} fusion(f32[32,128,128]{2,1,0:T(8,128)S(1)} %turn.2, f32[32,128,128]{2,1,0:T(8,128)} %copy-done), kind=kLoop, calls=%fused_computation.2 | loop fusion | flops 1048576 | bytes 8388608 | tf_op jit(solution)/shard_map/concatenate | solution.py:353
  79.2 6.7 %collective-permute-done.4.refs_0_.refs_5_ = f32[6,272,128]{2,1,0:T(8,128)S(1)} collective-permute-done((f32[6,272,128]{2,1,0:T(8,128)}, f32[6,272,128]{2,1,0:T(8,128)S(1)}, u32[]{:S(2)}, u32[]{:S(2)}) %collective-permute-start.4) | collective-permute-done | bytes 835616 | tf_op jit(solution)/shard_map/ppermute | solution.py:368
  85.9 8.7 %collective-permute-done.5.refs_4_.refs_9_ = f32[6,272,128]{2,1,0:T(8,128)} collective-permute-done((f32[6,272,128]{2,1,0:T(8,128)}, f32[6,272,128]{2,1,0:T(8,128)}, u32[]{:S(2)}, u32[]{:S(2)}) %collective-permute-start.5) | collective-permute-done | bytes 835616 | tf_op jit(solution)/shard_map/ppermute | solution.py:369
  94.6 21.1 %iterate.3.refs_2_ = f32[32,256,128]{2,1,0:T(8,128)} custom-call(f32[6,272,128]{2,1,0:T(8,128)S(1)} %collective-permute-done.4.refs_0_.refs_5_, f32[32,8,128]{2,1,0:T(8,128)S(1)} %collective-permute-done.1.refs_1_.refs_6_, f32[32,256,128]{2,1,0:T(8,128)} %pad_maximum_fusion.refs_2_.refs_7_, f32[32,8,128]{2,1,0:T(8,128)S(1)} %collective-permute-done.3.refs_3_.refs_8_, ...), custom_call_target="tpu_custom_call" | custom-call | flops 107233280 | bytes 18382848 | tf_op jit(solution)/shard_map/iterate/pallas_call | solution.py:259
  116.7 1.9 collective-permute-start.7
  120.1 3.6 %collective-permute-start.8 = (f32[32,8,128]{2,1,0:T(8,128)S(1)}, f32[32,8,128]{2,1,0:T(8,128)S(1)}, u32[]{:S(2)}, u32[]{:S(2)}) collective-permute-start(f32[32,8,128]{2,1,0:T(8,128)S(1)} %get-tuple-element.36), channel_id=1, source_target_pairs={{64,0},{2,1},{66,2},{4,3},{68,4},{6,5},{70,6},{65,64},{1,65},{67,6... | collective-permute-start | bytes 393224 | tf_op jit(solution)/shard_map/ppermute | solution.py:363
  123.7 3.2 %collective-permute-done.8.refs_3_ = f32[32,8,128]{2,1,0:T(8,128)S(1)} collective-permute-done((f32[32,8,128]{2,1,0:T(8,128)S(1)}, f32[32,8,128]{2,1,0:T(8,128)S(1)}, u32[]{:S(2)}, u32[]{:S(2)}) %collective-permute-start.8) | collective-permute-done | bytes 131104 | tf_op jit(solution)/shard_map/ppermute | solution.py:363
  127.0 1.9 collective-permute-start.9
  129.0 3.9 %collective-permute-start.10 = (f32[6,272,128]{2,1,0:T(8,128)S(1)}, f32[6,272,128]{2,1,0:T(8,128)S(1)}, u32[]{:S(2)}, u32[]{:S(2)}) collective-permute-start(f32[6,272,128]{2,1,0:T(8,128)S(1)} %pad_maximum_fusion.4), channel_id=1, source_target_pairs={{8,0},{16,8},{24,16},{32,24},{40,32},{48,40},{56,48},{9,1},{17,9},... | collective-permute-start | bytes 2506760 | tf_op jit(solution)/shard_map/ppermute | solution.py:369
  132.9 17.2 %collective-permute-done.9.refs_0_ = f32[6,272,128]{2,1,0:T(8,128)S(1)} collective-permute-done((f32[6,272,128]{2,1,0:T(8,128)S(1)}, f32[6,272,128]{2,1,0:T(8,128)S(1)}, u32[]{:S(2)}, u32[]{:S(2)}) %collective-permute-start.9) | collective-permute-done | bytes 835616 | tf_op jit(solution)/shard_map/ppermute | solution.py:368
  150.1 5.6 %collective-permute-done.10.refs_4_ = f32[6,272,128]{2,1,0:T(8,128)S(1)} collective-permute-done((f32[6,272,128]{2,1,0:T(8,128)S(1)}, f32[6,272,128]{2,1,0:T(8,128)S(1)}, u32[]{:S(2)}, u32[]{:S(2)}) %collective-permute-start.10) | collective-permute-done | bytes 835616 | tf_op jit(solution)/shard_map/ppermute | solution.py:369
  155.7 14.3 %iterate.5.refs_0_ = f32[64,32,128]{2,1,0:T(8,128)S(1)} custom-call(f32[6,272,128]{2,1,0:T(8,128)S(1)} %collective-permute-done.9.refs_0_, f32[32,8,128]{2,1,0:T(8,128)S(1)} %collective-permute-done.7.refs_1_, f32[32,256,128]{2,1,0:T(8,128)} %iterate.3.refs_2_, f32[32,8,128]{2,1,0:T(8,128)S(1)} %collective-permute-done.8.refs_3_, ...), custom_call_target="tpu_custom_call" | custom-call | flops 56770560 | bytes 9732096 | tf_op jit(solution)/shard_map/iterate/pallas_call | solution.py:259
  170.1 14.3 %iterate.4.refs_0_ = f32[64,32,128]{2,1,0:T(8,128)S(1)} custom-call(f32[6,272,128]{2,1,0:T(8,128)S(1)} %collective-permute-done.9.refs_0_, f32[32,8,128]{2,1,0:T(8,128)S(1)} %collective-permute-done.7.refs_1_, f32[32,256,128]{2,1,0:T(8,128)} %iterate.3.refs_2_, f32[32,8,128]{2,1,0:T(8,128)S(1)} %collective-permute-done.8.refs_3_, ...), custom_call_target="tpu_custom_call" | custom-call | flops 56770560 | bytes 9732096 | tf_op jit(solution)/shard_map/iterate/pallas_call | solution.py:259
  184.5 2.1 collective-permute-start.11
  186.6 1.5 place.4.refs_1_
  188.1 1.5 place.5.refs_1_
  189.6 6.7 %collective-permute-done.12.refs_0_ = f32[64,32,128]{2,1,0:T(8,128)} collective-permute-done((f32[64,32,128]{2,1,0:T(8,128)S(1)}, f32[64,32,128]{2,1,0:T(8,128)}, u32[]{:S(2)}, u32[]{:S(2)}) %collective-permute-start.12) | collective-permute-done | bytes 1048608 | tf_op jit(solution)/shard_map/ppermute | solution.py:391
  196.3 3.4 %place.6.refs_1_ = f32[64,32,512]{2,1,0:T(8,128)} custom-call(s32[1]{0:T(128)} %bitcast.9.where_ref, f32[64,32,128]{2,1,0:T(8,128)} %collective-permute-done.12.refs_0_, f32[64,32,512]{2,1,0:T(8,128)} %place.5.refs_1_), custom_call_target="tpu_custom_call", output_to_operand_aliasing={{}: (2, {})} | custom-call | bytes 2097152 | tf_op jit(solution)/shard_map/place/pallas_call | solution.py:296
  199.6 17.9 %collective-permute-done.11.refs_0_ = f32[64,32,128]{2,1,0:T(8,128)S(1)} collective-permute-done((f32[64,32,128]{2,1,0:T(8,128)S(1)}, f32[64,32,128]{2,1,0:T(8,128)S(1)}, u32[]{:S(2)}, u32[]{:S(2)}) %collective-permute-start.11) | collective-permute-done | bytes 1048608 | tf_op jit(solution)/shard_map/ppermute | solution.py:391
  217.5 1.5 place.7
  (41 shorter events, 9.7 us)
Async XLA Ops:
  0.0 4.8 %copy-start.1 = (f32[1,7]{1,0:T(1,128)S(1)}, f32[1,7]{1,0:T(1,128)}, u32[]{:S(2)}) copy-start(f32[1,7]{1,0:T(1,128)} %param.11) | copy-start | bytes 88
  0.0 5.4 %copy-start.2 = (f32[1,7]{1,0:T(1,128)S(1)}, f32[1,7]{1,0:T(1,128)}, u32[]{:S(2)}) copy-start(f32[1,7]{1,0:T(1,128)} %param.10) | copy-start | bytes 88
  0.0 6.1 %copy-start.3 = (f32[1,21]{1,0:T(1,128)S(1)}, f32[1,21]{1,0:T(1,128)}, u32[]{:S(2)}) copy-start(f32[1,21]{1,0:T(1,128)} %param.9) | copy-start | bytes 256
  2.7 26.0 %collective-permute-start = (f32[64,32,128]{2,1,0:T(8,128)S(1)}, f32[64,32,128]{2,1,0:T(8,128)S(1)}, u32[]{:S(2)}, u32[]{:S(2)}) collective-permute-start(f32[64,32,128]{2,1,0:T(8,128)S(1)} %get-tuple-element.39), channel_id=1, source_target_pairs={{0,64},{64,0},{1,65},{65,1},{2,66},{66,2},{3,67},{67,3},{4,68},{68... | collective-permute-start | bytes 3145736 | tf_op jit(solution)/shard_map/ppermute | solution.py:336
  4.7 46.7 %collective-permute-start.2 = (f32[64,32,128]{2,1,0:T(8,128)}, f32[64,32,128]{2,1,0:T(8,128)}, u32[]{:S(2)}, u32[]{:S(2)}) collective-permute-start(f32[64,32,128]{2,1,0:T(8,128)} %get-tuple-element.40), channel_id=1, source_target_pairs={{0,64},{64,0},{1,65},{65,1},{2,66},{66,2},{3,67},{67,3},{4,68},{68... | collective-permute-start | bytes 3145736 | tf_op jit(solution)/shard_map/ppermute | solution.py:336
  32.0 24.8 %collective-permute-start.1 = (f32[32,8,128]{2,1,0:T(8,128)S(1)}, f32[32,8,128]{2,1,0:T(8,128)S(1)}, u32[]{:S(2)}, u32[]{:S(2)}) collective-permute-start(f32[32,8,128]{2,1,0:T(8,128)S(1)} %slice.109), channel_id=1, source_target_pairs={{0,64},{1,2},{2,66},{3,4},{4,68},{5,6},{6,70},{64,65},{65,1},{66,6... | collective-permute-start | bytes 393224 | tf_op jit(solution)/shard_map/ppermute | solution.py:362
  54.7 14.3 %copy-start = (f32[32,128,128]{2,1,0:T(8,128)}, f32[32,128,128]{2,1,0:T(8,128)S(1)}, u32[]{:S(2)}) copy-start(f32[32,128,128]{2,1,0:T(8,128)S(1)} %turn.3) | copy-start | bytes 6291460
  54.7 6.9 %collective-permute-start.3 = (f32[32,8,128]{2,1,0:T(8,128)S(1)}, f32[32,8,128]{2,1,0:T(8,128)S(1)}, u32[]{:S(2)}, u32[]{:S(2)}) collective-permute-start(f32[32,8,128]{2,1,0:T(8,128)S(1)} %slice.113), channel_id=1, source_target_pairs={{64,0},{2,1},{66,2},{4,3},{68,4},{6,5},{70,6},{65,64},{1,65},{67,6... | collective-permute-start | bytes 393224 | tf_op jit(solution)/shard_map/ppermute | solution.py:363
  62.5 23.4 %collective-permute-start.4 = (f32[6,272,128]{2,1,0:T(8,128)}, f32[6,272,128]{2,1,0:T(8,128)S(1)}, u32[]{:S(2)}, u32[]{:S(2)}) collective-permute-start(f32[6,272,128]{2,1,0:T(8,128)} %pad_maximum_fusion.1), channel_id=1, source_target_pairs={{0,8},{8,16},{16,24},{24,32},{32,40},{40,48},{48,56},{1,9},{9,17},... | collective-permute-start | bytes 2506760 | tf_op jit(solution)/shard_map/ppermute | solution.py:368
  68.9 25.6 %collective-permute-start.5 = (f32[6,272,128]{2,1,0:T(8,128)}, f32[6,272,128]{2,1,0:T(8,128)}, u32[]{:S(2)}, u32[]{:S(2)}) collective-permute-start(f32[6,272,128]{2,1,0:T(8,128)} %pad_maximum_fusion.2), channel_id=1, source_target_pairs={{8,0},{16,8},{24,16},{32,24},{40,32},{48,40},{56,48},{9,1},{17,9},... | collective-permute-start | bytes 2506760 | tf_op jit(solution)/shard_map/ppermute | solution.py:369
  70.9 3.6 %collective-permute-start.6 = (f32[35]{0:T(128)S(1)}, f32[35]{0:T(128)S(1)}, u32[]{:S(2)}, u32[]{:S(2)}) collective-permute-start(f32[35]{0:T(128)S(1)} %pad_maximum_fusion.7), channel_id=1, source_target_pairs={{0,64},{64,0},{1,65},{65,1},{2,66},{66,2},{3,67},{67,3},{4,68},{68... | collective-permute-start | bytes 428 | tf_op jit(solution)/shard_map/ppermute | solution.py:340
  116.7 7.1 %collective-permute-start.7 = (f32[32,8,128]{2,1,0:T(8,128)S(1)}, f32[32,8,128]{2,1,0:T(8,128)S(1)}, u32[]{:S(2)}, u32[]{:S(2)}) collective-permute-start(f32[32,8,128]{2,1,0:T(8,128)S(1)} %get-tuple-element.35), channel_id=1, source_target_pairs={{0,64},{1,2},{2,66},{3,4},{4,68},{5,6},{6,70},{64,65},{65,1},{66,6... | collective-permute-start | bytes 393224 | tf_op jit(solution)/shard_map/ppermute | solution.py:362
  120.1 6.9 %collective-permute-start.8 = (f32[32,8,128]{2,1,0:T(8,128)S(1)}, f32[32,8,128]{2,1,0:T(8,128)S(1)}, u32[]{:S(2)}, u32[]{:S(2)}) collective-permute-start(f32[32,8,128]{2,1,0:T(8,128)S(1)} %get-tuple-element.36), channel_id=1, source_target_pairs={{64,0},{2,1},{66,2},{4,3},{68,4},{6,5},{70,6},{65,64},{1,65},{67,6... | collective-permute-start | bytes 393224 | tf_op jit(solution)/shard_map/ppermute | solution.py:363
  127.0 23.1 %collective-permute-start.9 = (f32[6,272,128]{2,1,0:T(8,128)S(1)}, f32[6,272,128]{2,1,0:T(8,128)S(1)}, u32[]{:S(2)}, u32[]{:S(2)}) collective-permute-start(f32[6,272,128]{2,1,0:T(8,128)S(1)} %pad_maximum_fusion.3), channel_id=1, source_target_pairs={{0,8},{8,16},{16,24},{24,32},{32,40},{40,48},{48,56},{1,9},{9,17},... | collective-permute-start | bytes 2506760 | tf_op jit(solution)/shard_map/ppermute | solution.py:368
  129.0 26.7 %collective-permute-start.10 = (f32[6,272,128]{2,1,0:T(8,128)S(1)}, f32[6,272,128]{2,1,0:T(8,128)S(1)}, u32[]{:S(2)}, u32[]{:S(2)}) collective-permute-start(f32[6,272,128]{2,1,0:T(8,128)S(1)} %pad_maximum_fusion.4), channel_id=1, source_target_pairs={{8,0},{16,8},{24,16},{32,24},{40,32},{48,40},{56,48},{9,1},{17,9},... | collective-permute-start | bytes 2506760 | tf_op jit(solution)/shard_map/ppermute | solution.py:369
  170.1 26.2 %collective-permute-start.12 = (f32[64,32,128]{2,1,0:T(8,128)S(1)}, f32[64,32,128]{2,1,0:T(8,128)}, u32[]{:S(2)}, u32[]{:S(2)}) collective-permute-start(f32[64,32,128]{2,1,0:T(8,128)S(1)} %iterate.5.refs_0_), channel_id=1, source_target_pairs={{0,64},{64,0},{1,65},{65,1},{2,66},{66,2},{3,67},{67,3},{4,68},{68... | collective-permute-start | bytes 3145736 | tf_op jit(solution)/shard_map/ppermute | solution.py:391
  184.5 33.1 %collective-permute-start.11 = (f32[64,32,128]{2,1,0:T(8,128)S(1)}, f32[64,32,128]{2,1,0:T(8,128)S(1)}, u32[]{:S(2)}, u32[]{:S(2)}) collective-permute-start(f32[64,32,128]{2,1,0:T(8,128)S(1)} %iterate.4.refs_0_), channel_id=1, source_target_pairs={{0,64},{64,0},{1,65},{65,1},{2,66},{66,2},{3,67},{67,3},{4,68},{68... | collective-permute-start | bytes 3145736 | tf_op jit(solution)/shard_map/ppermute | solution.py:391

commit v2 on v1

v2 whole, which is shorter than its diff:
```python
import functools

import jax
import jax.numpy as jnp
from jax import lax
from jax.experimental import pallas as pl
from jax.experimental.pallas import tpu as pltpu
from jax.sharding import PartitionSpec as P

ITERS = 2
Z = 64
LANES = 128
ROWS = 32
HALF = 256
CHUNK = 128
PAD = 6
SIDE = 8
MARGIN = 16
GROUP = 8
EXT_R = ROWS + 2 * PAD
EXT_C = HALF + 2 * MARGIN
VMEM_BYTES = 48 * 1024 * 1024
TINY = 1e-30


def params(**kwargs):
    return pltpu.CompilerParams(vmem_limit_bytes=VMEM_BYTES, **kwargs)


def blocks_of(total, largest=96):
    out, at = [], 0
    while at < total:
        size = min(largest, total - at)
        out.append((at, size))
        at += size
    return out


def matrices_kernel(kz_ref, blur_ref, adj_ref):
    taps = kz_ref.shape[0]
    lane = lax.broadcasted_iota(jnp.int32, (Z, LANES), 1)
    row = lax.broadcasted_iota(jnp.int32, (Z, LANES), 0)
    offset = row - lax.rem(lane, Z) + taps // 2
    mat = jnp.zeros((Z, LANES), jnp.float32)
    for t in range(taps):
        mat = mat + jnp.where(offset == t, kz_ref[t : t + 1, :], 0.0)
    high = mat.astype(jnp.bfloat16)
    low = (mat - high.astype(jnp.float32)).astype(jnp.bfloat16)
    blur_ref[0:Z, 0:LANES] = high
    blur_ref[0:Z, LANES:] = low
    blur_ref[Z:, 0:LANES] = high
    blur_ref[Z:, LANES:] = jnp.zeros((Z, LANES), jnp.bfloat16)
    adj = jnp.concatenate([mat, mat], axis=0).T * 0.5
    ahigh = adj.astype(jnp.bfloat16).astype(jnp.float32)
    alow = adj - ahigh
    first = lax.broadcasted_iota(jnp.int32, (LANES, LANES), 1) < Z
    adj_ref[0:LANES, :] = jnp.where(first, ahigh, alow).astype(jnp.bfloat16)
    adj_ref[LANES:, :] = jnp.where(first, ahigh, 0.0).astype(jnp.bfloat16)


def matrices(kz):
    return pl.pallas_call(
        matrices_kernel,
        out_shape=(
            jax.ShapeDtypeStruct((2 * Z, 2 * LANES), jnp.bfloat16),
            jax.ShapeDtypeStruct((2 * LANES, LANES), jnp.bfloat16),
        ),
        compiler_params=params(),
        name="matrices",
    )(kz)


def turn_kernel(where_ref, own_ref, other_ref, out_ref):
    own = own_ref.reshape(Z * GROUP, CHUNK)
    other = other_ref.reshape(Z * GROUP, CHUNK)
    first = where_ref[1] == 0
    for y in range(GROUP):
        mine = own[pl.ds(y, Z, stride=GROUP), :]
        theirs = other[pl.ds(y, Z, stride=GROUP), :]
        pair = jnp.concatenate(
            [jnp.where(first, mine, theirs), jnp.where(first, theirs, mine)], axis=0
        )
        out_ref[y] = pair.T


def turn(where, recorded, received, first_group, group_step):
    return pl.pallas_call(
        turn_kernel,
        out_shape=jax.ShapeDtypeStruct((2 * GROUP, HALF, LANES), jnp.float32),
        grid_spec=pltpu.PrefetchScalarGridSpec(
            num_scalar_prefetch=1,
            grid=(2, 2),
            in_specs=[
                pl.BlockSpec(
                    (1, Z, GROUP, CHUNK),
                    lambda i, j, w: (0, 0, first_group + group_step * i, 2 * w[0] + j),
                ),
                pl.BlockSpec((Z, GROUP, CHUNK), lambda i, j, w: (0, i, j)),
            ],
            out_specs=pl.BlockSpec((GROUP, CHUNK, LANES), lambda i, j, w: (i, j, 0)),
        ),
        cost_estimate=pl.CostEstimate(flops=0, bytes_accessed=4 << 20, transcendentals=0),
        compiler_params=params(),
        name="turn",
    )(where, recorded, received)


SPANS = ((0, PAD),) + tuple((PAD + GROUP * g, GROUP) for g in range(4)) + ((EXT_R - PAD, PAD),)
HOMES = ((0, 0), (1, 0), (1, GROUP), (0, GROUP))


def iterate_kernel(first, row0, n_out, *refs):
    n_in = n_out + 2 * PAD
    width = EXT_C if first else EXT_C - 2 * SIDE
    shift = 0 if first else SIDE
    inner = width - 2 * SIDE
    fold = (EXT_C - 2 * SIDE) // 2
    recorded, refs = refs[:8], refs[8:]
    if not first:
        field, refs = refs[:3], refs[3:]
    taps_ref, blur_ref, adj_ref = refs[:3]
    refs = refs[3:]
    if first:
        out_ref, top_ref, low_ref = refs[:3]
        refs = refs[3:]
    else:
        out_ref, refs = refs[0], refs[1:]
    r_buf, e_buf, xz_buf, xr_buf, pack, tmp, r_sem, e_sem = refs
    north, south = recorded[0], recorded[7]
    lower = lax.broadcasted_iota(jnp.int32, (width, LANES), 1) < Z

    def window(span, lo, hi):
        at, count = span
        a, b = max(at, lo), min(at + count, hi)
        return (a, b) if a < b else None

    def r_copies(k):
        got = window(SPANS[k], row0 + (0 if first else 3), row0 + n_in - (0 if first else 3))
        if got is None:
            return []
        a, b = got
        rows = pl.ds(a - row0, b - a)
        pairs = []
        if k in (0, 5):
            src = north if k == 0 else south
            pairs.append(
                (
                    src.at[pl.ds(a - SPANS[k][0], b - a), pl.ds(shift, width), :],
                    r_buf.at[rows, :, :],
                )
            )
        else:
            home, base = HOMES[k - 1]
            west, mid, east = recorded[1 + 3 * home : 4 + 3 * home]
            for src, lo, hi in (
                (west, 0, MARGIN),
                (mid, MARGIN, MARGIN + HALF),
                (east, MARGIN + HALF, EXT_C),
            ):
                c, d = max(lo, shift), min(hi, shift + width)
                pairs.append(
                    (
                        src.at[pl.ds(base + a - SPANS[k][0], b - a), pl.ds(c - lo, d - c), :],
                        r_buf.at[rows, pl.ds(c - shift, d - c), :],
                    )
                )
        return [
            pltpu.make_async_copy(src, dst, r_sem.at[k, n]) for n, (src, dst) in enumerate(pairs)
        ]

    def e_copies(k):
        got = window(SPANS[k], row0, row0 + n_in)
        if first or got is None:
            return []
        a, b = got
        at = a - SPANS[k][0]
        if k in (0, 5):
            src, dst = (field[0] if k == 0 else field[2]), pack.at[0 if k == 0 else 1]
            return [pltpu.make_async_copy(src, dst, e_sem.at[k])]
        src = field[1].at[pl.ds(GROUP * (k - 1) + at, b - a), :, :]
        return [pltpu.make_async_copy(src, e_buf.at[pl.ds(a - row0, b - a), :, :], e_sem.at[k])]

    recorded_in = [r_copies(k) for k in range(6)]
    field_in = [e_copies(k) for k in range(6)]
    for group in field_in + recorded_in:
        for c in group:
            c.start()

    kx = [taps_ref[t : t + 1, :] for t in range(7)]
    ky = [taps_ref[8 + t : 9 + t, :] for t in range(7)]
    col_blocks = blocks_of(width)

    def cols_pass(slot, taps, dst_ref, row):
        for at, size in col_blocks:
            acc = taps[0] * tmp[slot, pl.ds(5 + at, size), :]
            for t in range(1, 7):
                acc = acc + taps[t] * tmp[slot, pl.ds(5 + t + at, size), :]
            dst_ref[row, pl.ds(at, size), :] = acc

    def blur_row(slot, row):
        if first:
            r = r_buf[row]
            e = (r + pltpu.roll(r, Z, 1)) * 0.5
            e_buf[row] = e
        else:
            e = e_buf[row]
        high = e.astype(jnp.bfloat16).astype(jnp.float32)
        split = jnp.where(lower, high, e - high).astype(jnp.bfloat16)
        both = jnp.dot(split, blur_ref[...], preferred_element_type=jnp.float32)
        tmp[slot, pl.ds(8, width), :] = both[:, :LANES] + both[:, LANES:]
        cols_pass(slot, kx, xz_buf, row)

    for slot in range(2):
        tmp[slot, pl.ds(0, 8), :] = jnp.zeros((8, LANES), jnp.float32)
        tmp[slot, pl.ds(8 + width, 8), :] = jnp.zeros((8, LANES), jnp.float32)

    for k in range(6):
        got = window(SPANS[k], row0, row0 + n_in)
        if got is None:
            continue
        for c in recorded_in[k] if first else field_in[k]:
            c.wait()
        base, count = got[0] - row0, got[1] - got[0]

        def body(i, carry, k=k, base=base):
            for slot in range(2):
                row = base + 2 * i + slot
                if not first and k in (0, 5):
                    packed = pack[0 if k == 0 else 1, 2 * i + slot]
                    turned = pltpu.roll(packed, Z, 1)
                    e_buf[row, pl.ds(0, fold), :] = jnp.where(lower[:fold], packed, turned)
                    e_buf[row, pl.ds(fold, fold), :] = jnp.where(lower[:fold], turned, packed)
                blur_row(slot, row)
            return carry

        lax.fori_loop(0, count // 2, body, 0)

    if not first:
        for group in recorded_in:
            for c in group:
                c.wait()

    def rows_pass(src_ref, taps, row, at, size):
        acc = taps[0] * src_ref[row - 3, pl.ds(at, size), :]
        for t in range(1, 7):
            acc = acc + taps[t] * src_ref[row - 3 + t, pl.ds(at, size), :]
        return acc

    def ratio_body(i, carry):
        for slot in range(2):
            row = 3 + 2 * i + slot
            for at, size in col_blocks:
                blurred = rows_pass(xz_buf, ky, row, at, size)
                ratio = r_buf[row, pl.ds(at, size), :] / jnp.maximum(blurred, TINY)
                tmp[slot, pl.ds(8 + at, size), :] = ratio
            cols_pass(slot, kx[::-1], xr_buf, row)
        return carry

    lax.fori_loop(0, (n_in - 6) // 2, ratio_body, 0)

    def update_row(row):
        spread = []
        for at, size in blocks_of(inner, 64):
            spread.append(rows_pass(xr_buf, ky[::-1], row, SIDE + at, size))
        spread = jnp.concatenate(spread, axis=0)
        high = spread.astype(jnp.bfloat16)
        low = (spread - high.astype(jnp.float32)).astype(jnp.bfloat16)
        both = jnp.dot(
            jnp.concatenate([high, low], axis=1), adj_ref[...], preferred_element_type=jnp.float32
        )
        factor = both + pltpu.roll(both, Z, 1)
        return e_buf[row, pl.ds(SIDE, inner), :] * factor

    def update_body(i, carry, base=0):
        for k in range(2):
            y = base + 2 * i + k
            new = update_row(PAD + y)
            if first:
                out_ref[y] = new
            else:
                for j in range(2):
                    flat = out_ref.at[j].reshape(Z * GROUP, CHUNK)
                    flat[pl.ds(y, Z, stride=GROUP), :] = new[j * CHUNK : (j + 1) * CHUNK].T[:Z]
        return carry

    lax.fori_loop(0, n_out // 2, update_body, 0)
    if first:
        for y in range(PAD):
            for ref, row in ((top_ref, y), (low_ref, ROWS - PAD + y)):
                ref[y] = jnp.where(
                    lower[:fold], out_ref[row, pl.ds(0, fold), :], out_ref[row, pl.ds(fold, fold), :]
                )


def iterate(recorded, field, taps, blur, adj, *, first, row0, n_out):
    n_in = n_out + 2 * PAD
    width = EXT_C if first else EXT_C - 2 * SIDE
    fold = (EXT_C - 2 * SIDE) // 2
    if first:
        edge = jax.ShapeDtypeStruct((PAD, fold, LANES), jnp.float32)
        out = (jax.ShapeDtypeStruct((ROWS, EXT_C - 2 * SIDE, LANES), jnp.float32), edge, edge)
        out_specs = (pl.BlockSpec(memory_space=pltpu.VMEM),) * 3
        pieces = list(recorded)
    else:
        out = jax.ShapeDtypeStruct((2, Z, GROUP, CHUNK), jnp.float32)
        out_specs = pl.BlockSpec(memory_space=pltpu.VMEM)
        pieces = list(recorded) + list(field)
    row = pltpu.VMEM((n_in, width, LANES), jnp.float32)
    vregs = n_in * width // 8
    return pl.pallas_call(
        functools.partial(iterate_kernel, first, row0, n_out),
        out_shape=out,
        in_specs=[pl.BlockSpec(memory_space=pl.ANY)] * len(pieces)
        + [pl.BlockSpec(memory_space=pltpu.VMEM)] * 3,
        out_specs=out_specs,
        scratch_shapes=[
            row,
            row,
            row,
            row,
            pltpu.VMEM((2, PAD, fold, LANES), jnp.float32),
            pltpu.VMEM((2, width + 16, LANES), jnp.float32),
            pltpu.SemaphoreType.DMA((6, 3)),
            pltpu.SemaphoreType.DMA((6,)),
        ],
        cost_estimate=pl.CostEstimate(
            flops=vregs * 1024 * 70, bytes_accessed=vregs * 4096 * 3, transcendentals=0
        ),
        compiler_params=params(),
        name="iterate",
    )(*pieces, taps, blur, adj)


def place_kernel(where_ref, *refs):
    refs[-1][...] = refs[0][0]


def place(where, block, whole, group):
    args = [where, block]
    in_specs = [pl.BlockSpec((1, Z, GROUP, CHUNK), lambda j, w: (j, 0, 0, 0))]
    aliases = {}
    if whole is not None:
        args.append(whole)
        in_specs.append(pl.BlockSpec(memory_space=pl.ANY))
        aliases = {2: 0}
    return pl.pallas_call(
        place_kernel,
        out_shape=jax.ShapeDtypeStruct((Z, ROWS, 2 * HALF), jnp.float32),
        grid_spec=pltpu.PrefetchScalarGridSpec(
            num_scalar_prefetch=1,
            grid=(2,),
            in_specs=in_specs,
            out_specs=pl.BlockSpec((Z, GROUP, CHUNK), lambda j, w: (0, group, 2 * w[0] + j)),
        ),
        input_output_aliases=aliases,
        cost_estimate=pl.CostEstimate(flops=0, bytes_accessed=1 << 20, transcendentals=0),
        compiler_params=params(),
        name="place",
    )(*args)


def neighbours(views, tiles):
    right = []
    for v in range(views):
        for t in range(tiles):
            if (t + v) % 2 == 0:
                right.append((v * tiles + t, (1 - v) * tiles + t))
            elif t + 1 < tiles:
                right.append((v * tiles + t, v * tiles + t + 1))
    return right


def per_device(views_data, psf_axial, psf_rows, psf_cols):
    views, tiles, bands = lax.axis_size("view"), lax.axis_size("tx"), lax.axis_size("ty")
    swap = [(0, 1), (1, 0)]
    right = neighbours(views, tiles)
    left = [(b, a) for a, b in right]
    down = [(i, i + 1) for i in range(bands - 1)]
    up = [(b, a) for a, b in down]
    half = lax.rem(lax.axis_index("tx") + lax.axis_index("view"), 2)

    def other_rows(*starts):
        at = (1 - half) * HALF
        return jnp.concatenate(
            [
                lax.dynamic_slice(views_data, (0, 0, row, at), (1, Z, rows, HALF))[0]
                for row, rows in starts
            ],
            axis=1,
        )

    border_in = lax.ppermute(other_rows((0, GROUP), (ROWS - GROUP, GROUP)), "view", swap)
    inner_in = lax.ppermute(other_rows((GROUP, 2 * GROUP)), "view", swap)

    norm = lambda k: k[0] / jnp.sum(k[0])
    own = jnp.concatenate([norm(psf_axial), norm(psf_rows), norm(psf_cols)])
    other = lax.ppermute(own, "view", swap)
    view = lax.axis_index("view")
    lanes = jnp.concatenate(
        [
            jnp.broadcast_to(jnp.where(view == 0, own, other)[:, None], (own.shape[0], Z)),
            jnp.broadcast_to(jnp.where(view == 0, other, own)[:, None], (own.shape[0], Z)),
        ],
        axis=1,
    )
    blur, adj = matrices(lanes[:21])
    taps = jnp.zeros((16, LANES), jnp.float32)
    taps = taps.at[0:7].set(lanes[28:35]).at[8:15].set(lanes[21:28])

    where = jnp.stack([half, view]).astype(jnp.int32)
    there = (1 - half).astype(jnp.int32)[None]

    def widen(block):
        west = lax.ppermute(block[:, HALF - MARGIN :], ("view", "tx"), right)
        east = lax.ppermute(block[:, :MARGIN], ("view", "tx"), left)
        return west, block, east

    border = widen(turn(where, views_data, border_in, 0, 3))

    def edge(rows):
        return jnp.concatenate([part[rows] for part in border], axis=1)

    north = lax.ppermute(edge(slice(2 * GROUP - PAD, 2 * GROUP)), "ty", down)
    south = lax.ppermute(edge(slice(0, PAD)), "ty", up)
    inner = widen(turn(where, views_data, inner_in, 1, 1))
    recorded = (north,) + border + inner + (south,)

    estimate, top, low = iterate(
        recorded, None, taps, blur, adj, first=True, row0=0, n_out=ROWS
    )
    field = (lax.ppermute(low, "ty", down), estimate, lax.ppermute(top, "ty", up))
    whole = None
    theirs = []
    for group in (1, 2, 0, 3):
        block = iterate(
            recorded, field, taps, blur, adj, first=False, row0=GROUP * group, n_out=GROUP
        )
        theirs.append((group, lax.ppermute(block, "view", swap)))
        whole = place(where[:1], block, whole, group)
    for group, block in theirs:
        whole = place(there, block, whole, group)
    return whole


def solution(mesh):
    placed = (P("view", None, "ty", "tx"), P("view", None), P("view", None), P("view", None))
    return jax.shard_map(
        per_device, mesh=mesh, in_specs=placed, out_specs=P(None, "ty", "tx"), check_vma=False
    )
```

time: 220 us -> 182 us (0.83)
  waiting for transfers between devices: 110 us -> 66.7 us
  other arithmetic: 10.5 us -> 6.09 us
  local copies, waits for them, and re-layouts: 5.47 us -> 8.89 us
  starting transfers between devices: 28.8 us -> 32.1 us
  Pallas kernels: 64.3 us -> 66.9 us
    ppermute x12 -> x14, waiting for transfers between devices: 106 us -> 64.2 us  [the longest x1 18 us: per_device(): lax.ppermute(other_rows((0, GROUP), (ROWS - GROUP, GROUP)), 'view', swap)]
    unnamed x8 -> x18, local copies, waits for them, and re-layouts: 0.02 us -> 4.24 us
    pallas_call x5 -> x7, Pallas kernels: 56.2 us -> 60.3 us  [the longest x5 53.5 us: iterate(): pl.pallas_call(functools.partial(iterate_kernel, first, row0, n_out), out...]
    concatenate x6 -> x3, other arithmetic: 6.12 us -> 2.03 us  [the longest x2 1.95 us: edge(): return jnp.concatenate([part[rows] for part in border], axis=1)]
    ppermute x12 -> x14, starting transfers between devices: 28.7 us -> 31.1 us  [the longest x2 7.77 us: widen(): west = lax.ppermute(block[:, HALF - MARGIN:], ('view', 'tx'), right)]
    pallas_call x4 -> x8, Pallas kernels: 7.93 us -> 6.45 us  [place(): pl.pallas_call(place_kernel, out_shape=jax.ShapeDtypeStruct((Z, ROWS, 2 *...]
  transfers between devices with their start and end apart: 13 -> 15, of which waited for: 11 -> 11; matrix products, arithmetic and copies ran while one was open for 5% -> 5% of each run, Pallas kernels for 12% -> 20%
where the time goes in v2:
time: 182 us; the launch traced here: 181 us
  Pallas kernels  66.9 us (37%)
  waiting for transfers between devices  66.7 us (37%)
  starting transfers between devices  32.1 us (18%)
  local copies, waits for them, and re-layouts  8.89 us (5%)
  other arithmetic  6.09 us (3%)
    pallas_call x5, Pallas kernels, iterate(): pl.pallas_call(functools.partial(iterate_kernel, first, row0, n_out), out...  53.5 us
    ppermute x1, waiting for transfers between devices, per_device(): lax.ppermute(other_rows((0, GROUP), (ROWS - GROUP, GROUP)), 'view', swap)  18 us
    ppermute x2, waiting for transfers between devices, widen(): west = lax.ppermute(block[:, HALF - MARGIN:], ('view', 'tx'), right)  15.3 us
    ppermute x4, waiting for transfers between devices, per_device(): theirs.append((group, lax.ppermute(block, 'view', swap)))  11.6 us
    ppermute x2, starting transfers between devices, widen(): west = lax.ppermute(block[:, HALF - MARGIN:], ('view', 'tx'), right)  7.77 us
    ppermute x1, waiting for transfers between devices, per_device(): lax.ppermute(top, 'ty', up)  6.89 us
    pallas_call x2, Pallas kernels, turn(): pl.pallas_call(turn_kernel, out_shape=jax.ShapeDtypeStruct((2 * GROUP, HA...  6.79 us
    pallas_call x8, Pallas kernels, place(): pl.pallas_call(place_kernel, out_shape=jax.ShapeDtypeStruct((Z, ROWS, 2 *...  6.45 us
  transfers between devices with their start and end apart: 15, of which 11 were waited for; matrix products, arithmetic and copies ran while one was open for 5% of the time, Pallas kernels for 20%

profile of v2, /device:TPU:26, one launch (start us, length us, event | category | flops | bytes accessed | tf_op | source)
XLA Modules:
  0.0 181.0 jit_solution(10142874398938598898)
XLA Ops:
  0.0 1.3 dynamic-slice_bitcast_fusion.2
  1.4 2.0 %collective-permute-start = (f32[64,16,256]{2,1,0:T(8,128)S(1)}, f32[64,16,256]{2,1,0:T(8,128)S(1)}, u32[]{:S(2)}, u32[]{:S(2)}) collective-permute-start(f32[64,16,256]{2,1,0:T(8,128)S(1)} %pad_maximum_fusion), channel_id=1, source_target_pairs={{0,64},{64,0},{1,65},{65,1},{2,66},{66,2},{3,67},{67,3},{4,68},{68... | collective-permute-start | bytes 3145736 | tf_op jit(solution)/shard_map/ppermute | solution.py:392
  3.4 2.3 %dynamic-slice_bitcast_fusion = f32[64,16,256]{2,1,0:T(8,128)} fusion(f32[1,64,32,512]{3,2,1,0:T(8,128)} %own_ref.3, s32[]{:T(128)S(6)} %select_n.17), kind=kLoop, calls=%fused_computation.1 | loop fusion | bytes 2097156 | tf_op jit(solution)/shard_map/squeeze | solution.py:386
  8.3 1.2 divide_bitcast_fusion
  9.5 18.0 %collective-permute-done.other_ref = f32[64,16,256]{2,1,0:T(8,128)S(1)} collective-permute-done((f32[64,16,256]{2,1,0:T(8,128)S(1)}, f32[64,16,256]{2,1,0:T(8,128)S(1)}, u32[]{:S(2)}, u32[]{:S(2)}) %collective-permute-start) | collective-permute-done | bytes 1048608 | tf_op jit(solution)/shard_map/ppermute | solution.py:392
  27.5 3.3 %turn.2.refs_2_ = f32[16,256,128]{2,1,0:T(8,128)S(1)} custom-call(s32[2]{0:T(128)S(1)} %pad_add_fusion.where_ref, f32[1,64,32,512]{3,2,1,0:T(8,128)} %own_ref.3, f32[64,16,256]{2,1,0:T(8,128)S(1)} %collective-permute-done.other_ref), custom_call_target="tpu_custom_call" | custom-call | bytes 4194304 | tf_op jit(solution)/shard_map/turn/pallas_call | solution.py:87
  30.9 3.8 %collective-permute-start.1 = (f32[16,16,128]{2,1,0:T(8,128)S(1)}, f32[16,16,128]{2,1,0:T(8,128)S(1)}, u32[]{:S(2)}, u32[]{:S(2)}) collective-permute-start(f32[16,16,128]{2,1,0:T(8,128)S(1)} %get-tuple-element.45), channel_id=1, source_target_pairs={{0,64},{1,2},{2,66},{3,4},{4,68},{5,6},{6,70},{64,65},{65,1},{66,6... | collective-permute-start | bytes 393224 | tf_op jit(solution)/shard_map/ppermute | solution.py:414
  34.8 1.9 %collective-permute-start.2 = (f32[16,16,128]{2,1,0:T(8,128)S(1)}, f32[16,16,128]{2,1,0:T(8,128)S(1)}, u32[]{:S(2)}, u32[]{:S(2)}) collective-permute-start(f32[16,16,128]{2,1,0:T(8,128)S(1)} %get-tuple-element.46), channel_id=1, source_target_pairs={{64,0},{2,1},{66,2},{4,3},{68,4},{6,5},{70,6},{65,64},{1,65},{67,6... | collective-permute-start | bytes 393224 | tf_op jit(solution)/shard_map/ppermute | solution.py:415
  36.8 14.3 %collective-permute-done.1.refs_1_ = f32[16,16,128]{2,1,0:T(8,128)S(1)} collective-permute-done((f32[16,16,128]{2,1,0:T(8,128)S(1)}, f32[16,16,128]{2,1,0:T(8,128)S(1)}, u32[]{:S(2)}, u32[]{:S(2)}) %collective-permute-start.1) | collective-permute-done | bytes 131104 | tf_op jit(solution)/shard_map/ppermute | solution.py:414
  51.9 1.0 pad_maximum_fusion.1
  52.8 5.3 %collective-permute-start.3 = (f32[6,288,128]{2,1,0:T(8,128)}, f32[6,288,128]{2,1,0:T(8,128)S(1)}, u32[]{:S(2)}, u32[]{:S(2)}) collective-permute-start(f32[6,288,128]{2,1,0:T(8,128)} %pad_maximum_fusion.1), channel_id=1, source_target_pairs={{0,8},{8,16},{16,24},{24,32},{32,40},{40,48},{48,56},{1,9},{9,17},... | collective-permute-start | bytes 2654216 | tf_op jit(solution)/shard_map/ppermute | solution.py:423
  59.1 1.9 %collective-permute-start.7 = (f32[6,288,128]{2,1,0:T(8,128)}, f32[6,288,128]{2,1,0:T(8,128)}, u32[]{:S(2)}, u32[]{:S(2)}) collective-permute-start(f32[6,288,128]{2,1,0:T(8,128)} %pad_maximum_fusion.2), channel_id=1, source_target_pairs={{8,0},{16,8},{24,16},{32,24},{40,32},{48,40},{56,48},{9,1},{17,9},... | collective-permute-start | bytes 2654216 | tf_op jit(solution)/shard_map/ppermute | solution.py:424
  61.1 1.1 collective-permute-start.8
  62.1 2.5 %collective-permute-done.8 = f32[35]{0:T(128)S(1)} collective-permute-done((f32[35]{0:T(128)S(1)}, f32[35]{0:T(128)S(1)}, u32[]{:S(2)}, u32[]{:S(2)}) %collective-permute-start.8) | collective-permute-done | bytes 172 | tf_op jit(solution)/shard_map/ppermute | solution.py:397
  64.9 3.5 %turn.3.refs_5_ = f32[16,256,128]{2,1,0:T(8,128)S(1)} custom-call(s32[2]{0:T(128)S(1)} %pad_add_fusion.where_ref, f32[1,64,32,512]{3,2,1,0:T(8,128)} %own_ref.3, f32[64,16,256]{2,1,0:T(8,128)} %collective-permute-done.4.other_ref), custom_call_target="tpu_custom_call" | custom-call | bytes 4194304 | tf_op jit(solution)/shard_map/turn/pallas_call | solution.py:87
  68.4 1.3 copy-done
  70.5 1.9 %collective-permute-start.6 = (f32[16,16,128]{2,1,0:T(8,128)}, f32[16,16,128]{2,1,0:T(8,128)S(1)}, u32[]{:S(2)}, u32[]{:S(2)}) collective-permute-start(f32[16,16,128]{2,1,0:T(8,128)} %get-tuple-element.43), channel_id=1, source_target_pairs={{64,0},{2,1},{66,2},{4,3},{68,4},{6,5},{70,6},{65,64},{1,65},{67,6... | collective-permute-start | bytes 393224 | tf_op jit(solution)/shard_map/ppermute | solution.py:415
  72.4 3.9 %collective-permute-start.5 = (f32[16,16,128]{2,1,0:T(8,128)}, f32[16,16,128]{2,1,0:T(8,128)S(1)}, u32[]{:S(2)}, u32[]{:S(2)}) collective-permute-start(f32[16,16,128]{2,1,0:T(8,128)} %get-tuple-element.44), channel_id=1, source_target_pairs={{0,64},{1,2},{2,66},{3,4},{4,68},{5,6},{6,70},{64,65},{65,1},{66,6... | collective-permute-start | bytes 393224 | tf_op jit(solution)/shard_map/ppermute | solution.py:414
  79.1 6.1 %collective-permute-done.7.refs_7_ = f32[6,288,128]{2,1,0:T(8,128)} collective-permute-done((f32[6,288,128]{2,1,0:T(8,128)}, f32[6,288,128]{2,1,0:T(8,128)}, u32[]{:S(2)}, u32[]{:S(2)}) %collective-permute-start.7) | collective-permute-done | bytes 884768 | tf_op jit(solution)/shard_map/ppermute | solution.py:424
  86.9 22.0 %iterate.5 = (f32[32,272,128]{2,1,0:T(8,128)}, f32[6,136,128]{2,1,0:T(8,128)S(1)}, f32[6,136,128]{2,1,0:T(8,128)S(1)}) custom-call(f32[6,288,128]{2,1,0:T(8,128)S(1)} %collective-permute-done.3.refs_0_, f32[16,16,128]{2,1,0:T(8,128)S(1)} %collective-permute-done.1.refs_1_, f32[16,256,128]{2,1,0:T(8,128)S(1)} %turn.2.refs_2_, ...), custom_call_target="tpu_custom_call" | custom-call | flops 113541120 | bytes 19464192 | tf_op jit(solution)/shard_map/iterate/pallas_call | solution.py:310
  109.0 1.9 %collective-permute-start.9 = (f32[6,136,128]{2,1,0:T(8,128)S(1)}, f32[6,136,128]{2,1,0:T(8,128)S(1)}, u32[]{:S(2)}, u32[]{:S(2)}) collective-permute-start(f32[6,136,128]{2,1,0:T(8,128)S(1)} %get-tuple-element.36), channel_id=1, source_target_pairs={{0,8},{8,16},{16,24},{24,32},{32,40},{40,48},{48,56},{1,9},{9,17},... | collective-permute-start | bytes 1253384 | tf_op jit(solution)/shard_map/ppermute | solution.py:431
  110.9 3.9 %collective-permute-start.10 = (f32[6,136,128]{2,1,0:T(8,128)S(1)}, f32[6,136,128]{2,1,0:T(8,128)S(1)}, u32[]{:S(2)}, u32[]{:S(2)}) collective-permute-start(f32[6,136,128]{2,1,0:T(8,128)S(1)} %get-tuple-element.38), channel_id=1, source_target_pairs={{8,0},{16,8},{24,16},{32,24},{40,32},{48,40},{56,48},{9,1},{17,9},... | collective-permute-start | bytes 1253384 | tf_op jit(solution)/shard_map/ppermute | solution.py:431
  114.8 5.3 %collective-permute-done.9.refs_8_ = f32[6,136,128]{2,1,0:T(8,128)S(1)} collective-permute-done((f32[6,136,128]{2,1,0:T(8,128)S(1)}, f32[6,136,128]{2,1,0:T(8,128)S(1)}, u32[]{:S(2)}, u32[]{:S(2)}) %collective-permute-start.9) | collective-permute-done | bytes 417824 | tf_op jit(solution)/shard_map/ppermute | solution.py:431
  120.1 6.9 %collective-permute-done.10.refs_10_ = f32[6,136,128]{2,1,0:T(8,128)S(1)} collective-permute-done((f32[6,136,128]{2,1,0:T(8,128)S(1)}, f32[6,136,128]{2,1,0:T(8,128)S(1)}, u32[]{:S(2)}, u32[]{:S(2)}) %collective-permute-start.10) | collective-permute-done | bytes 417824 | tf_op jit(solution)/shard_map/ppermute | solution.py:431
  127.0 7.4 %iterate.7.refs_0_ = f32[2,64,8,128]{3,2,1,0:T(8,128)S(1)} custom-call(f32[6,288,128]{2,1,0:T(8,128)S(1)} %collective-permute-done.3.refs_0_, f32[16,16,128]{2,1,0:T(8,128)S(1)} %collective-permute-done.1.refs_1_, f32[16,256,128]{2,1,0:T(8,128)S(1)} %turn.2.refs_2_, f32[16,16,128]{2,1,0:T(8,128)S(1)} %collective-permute-done.2.refs_3_, ...), custom_call_target="tpu_custom_call" | custom-call | flops 48742400 | bytes 8355840 | tf_op jit(solution)/shard_map/iterate/pallas_call | solution.py:310
  134.5 8.0 %iterate.8.refs_0_ = f32[2,64,8,128]{3,2,1,0:T(8,128)S(1)} custom-call(f32[6,288,128]{2,1,0:T(8,128)S(1)} %collective-permute-done.3.refs_0_, f32[16,16,128]{2,1,0:T(8,128)S(1)} %collective-permute-done.1.refs_1_, f32[16,256,128]{2,1,0:T(8,128)S(1)} %turn.2.refs_2_, f32[16,16,128]{2,1,0:T(8,128)S(1)} %collective-permute-done.2.refs_3_, ...), custom_call_target="tpu_custom_call" | custom-call | flops 48742400 | bytes 8355840 | tf_op jit(solution)/shard_map/iterate/pallas_call | solution.py:310
  142.5 2.1 %collective-permute-start.13 = (f32[2,64,8,128]{3,2,1,0:T(8,128)S(1)}, f32[2,64,8,128]{3,2,1,0:T(8,128)S(1)}, u32[]{:S(2)}, u32[]{:S(2)}) collective-permute-start(f32[2,64,8,128]{3,2,1,0:T(8,128)S(1)} %iterate.8.refs_0_), channel_id=1, source_target_pairs={{0,64},{64,0},{1,65},{65,1},{2,66},{66,2},{3,67},{67,3},{4,68},{68... | collective-permute-start | bytes 1572872 | tf_op jit(solution)/shard_map/ppermute | solution.py:438
  144.6 8.0 %iterate.9.refs_0_ = f32[2,64,8,128]{3,2,1,0:T(8,128)S(1)} custom-call(f32[6,288,128]{2,1,0:T(8,128)S(1)} %collective-permute-done.3.refs_0_, f32[16,16,128]{2,1,0:T(8,128)S(1)} %collective-permute-done.1.refs_1_, f32[16,256,128]{2,1,0:T(8,128)S(1)} %turn.2.refs_2_, f32[16,16,128]{2,1,0:T(8,128)S(1)} %collective-permute-done.2.refs_3_, ...), custom_call_target="tpu_custom_call" | custom-call | flops 48742400 | bytes 8355840 | tf_op jit(solution)/shard_map/iterate/pallas_call | solution.py:310
  152.7 8.2 %iterate.6.refs_0_ = f32[2,64,8,128]{3,2,1,0:T(8,128)S(1)} custom-call(f32[6,288,128]{2,1,0:T(8,128)S(1)} %collective-permute-done.3.refs_0_, f32[16,16,128]{2,1,0:T(8,128)S(1)} %collective-permute-done.1.refs_1_, f32[16,256,128]{2,1,0:T(8,128)S(1)} %turn.2.refs_2_, f32[16,16,128]{2,1,0:T(8,128)S(1)} %collective-permute-done.2.refs_3_, ...), custom_call_target="tpu_custom_call" | custom-call | flops 48742400 | bytes 8355840 | tf_op jit(solution)/shard_map/iterate/pallas_call | solution.py:310
  160.8 2.1 %collective-permute-start.11 = (f32[2,64,8,128]{3,2,1,0:T(8,128)S(1)}, f32[2,64,8,128]{3,2,1,0:T(8,128)S(1)}, u32[]{:S(2)}, u32[]{:S(2)}) collective-permute-start(f32[2,64,8,128]{3,2,1,0:T(8,128)S(1)} %iterate.6.refs_0_), channel_id=1, source_target_pairs={{0,64},{64,0},{1,65},{65,1},{2,66},{66,2},{3,67},{67,3},{4,68},{68... | collective-permute-start | bytes 1572872 | tf_op jit(solution)/shard_map/ppermute | solution.py:438
  166.1 5.7 %collective-permute-done.14.refs_0_ = f32[2,64,8,128]{3,2,1,0:T(8,128)S(1)} collective-permute-done((f32[2,64,8,128]{3,2,1,0:T(8,128)S(1)}, f32[2,64,8,128]{3,2,1,0:T(8,128)S(1)}, u32[]{:S(2)}, u32[]{:S(2)}) %collective-permute-start.14) | collective-permute-done | bytes 524320 | tf_op jit(solution)/shard_map/ppermute | solution.py:438
  174.3 5.9 %collective-permute-done.11.refs_0_ = f32[2,64,8,128]{3,2,1,0:T(8,128)S(1)} collective-permute-done((f32[2,64,8,128]{3,2,1,0:T(8,128)S(1)}, f32[2,64,8,128]{3,2,1,0:T(8,128)S(1)}, u32[]{:S(2)}, u32[]{:S(2)}) %collective-permute-start.11) | collective-permute-done | bytes 524320 | tf_op jit(solution)/shard_map/ppermute | solution.py:438
  (56 shorter events, 16.8 us)
Async XLA Ops:
  0.0 5.8 %copy-start.6 = (f32[1,7]{1,0:T(1,128)S(1)}, f32[1,7]{1,0:T(1,128)}, u32[]{:S(2)}) copy-start(f32[1,7]{1,0:T(1,128)} %param.11) | copy-start | bytes 88
  0.0 6.4 %copy-start.7 = (f32[1,7]{1,0:T(1,128)S(1)}, f32[1,7]{1,0:T(1,128)}, u32[]{:S(2)}) copy-start(f32[1,7]{1,0:T(1,128)} %param.10) | copy-start | bytes 88
  0.0 7.1 %copy-start.8 = (f32[1,21]{1,0:T(1,128)S(1)}, f32[1,21]{1,0:T(1,128)}, u32[]{:S(2)}) copy-start(f32[1,21]{1,0:T(1,128)} %param.9) | copy-start | bytes 256
  1.4 26.1 %collective-permute-start = (f32[64,16,256]{2,1,0:T(8,128)S(1)}, f32[64,16,256]{2,1,0:T(8,128)S(1)}, u32[]{:S(2)}, u32[]{:S(2)}) collective-permute-start(f32[64,16,256]{2,1,0:T(8,128)S(1)} %pad_maximum_fusion), channel_id=1, source_target_pairs={{0,64},{64,0},{1,65},{65,1},{2,66},{66,2},{3,67},{67,3},{4,68},{68... | collective-permute-start | bytes 3145736 | tf_op jit(solution)/shard_map/ppermute | solution.py:392
  5.7 59.2 %collective-permute-start.4 = (f32[64,16,256]{2,1,0:T(8,128)}, f32[64,16,256]{2,1,0:T(8,128)}, u32[]{:S(2)}, u32[]{:S(2)}) collective-permute-start(f32[64,16,256]{2,1,0:T(8,128)} %dynamic-slice_bitcast_fusion), channel_id=1, source_target_pairs={{0,64},{64,0},{1,65},{65,1},{2,66},{66,2},{3,67},{67,3},{4,68},{68... | collective-permute-start | bytes 3145736 | tf_op jit(solution)/shard_map/ppermute | solution.py:393
  30.9 20.2 %collective-permute-start.1 = (f32[16,16,128]{2,1,0:T(8,128)S(1)}, f32[16,16,128]{2,1,0:T(8,128)S(1)}, u32[]{:S(2)}, u32[]{:S(2)}) collective-permute-start(f32[16,16,128]{2,1,0:T(8,128)S(1)} %get-tuple-element.45), channel_id=1, source_target_pairs={{0,64},{1,2},{2,66},{3,4},{4,68},{5,6},{6,70},{64,65},{65,1},{66,6... | collective-permute-start | bytes 393224 | tf_op jit(solution)/shard_map/ppermute | solution.py:414
  34.8 17.0 %collective-permute-start.2 = (f32[16,16,128]{2,1,0:T(8,128)S(1)}, f32[16,16,128]{2,1,0:T(8,128)S(1)}, u32[]{:S(2)}, u32[]{:S(2)}) collective-permute-start(f32[16,16,128]{2,1,0:T(8,128)S(1)} %get-tuple-element.46), channel_id=1, source_target_pairs={{64,0},{2,1},{66,2},{4,3},{68,4},{6,5},{70,6},{65,64},{1,65},{67,6... | collective-permute-start | bytes 393224 | tf_op jit(solution)/shard_map/ppermute | solution.py:415
  52.8 26.3 %collective-permute-start.3 = (f32[6,288,128]{2,1,0:T(8,128)}, f32[6,288,128]{2,1,0:T(8,128)S(1)}, u32[]{:S(2)}, u32[]{:S(2)}) collective-permute-start(f32[6,288,128]{2,1,0:T(8,128)} %pad_maximum_fusion.1), channel_id=1, source_target_pairs={{0,8},{8,16},{16,24},{24,32},{32,40},{40,48},{48,56},{1,9},{9,17},... | collective-permute-start | bytes 2654216 | tf_op jit(solution)/shard_map/ppermute | solution.py:423
  59.1 26.2 %collective-permute-start.7 = (f32[6,288,128]{2,1,0:T(8,128)}, f32[6,288,128]{2,1,0:T(8,128)}, u32[]{:S(2)}, u32[]{:S(2)}) collective-permute-start(f32[6,288,128]{2,1,0:T(8,128)} %pad_maximum_fusion.2), channel_id=1, source_target_pairs={{8,0},{16,8},{24,16},{32,24},{40,32},{48,40},{56,48},{9,1},{17,9},... | collective-permute-start | bytes 2654216 | tf_op jit(solution)/shard_map/ppermute | solution.py:424
  61.1 3.6 %collective-permute-start.8 = (f32[35]{0:T(128)S(1)}, f32[35]{0:T(128)S(1)}, u32[]{:S(2)}, u32[]{:S(2)}) collective-permute-start(f32[35]{0:T(128)S(1)} %pad_maximum_fusion.5), channel_id=1, source_target_pairs={{0,64},{64,0},{1,65},{65,1},{2,66},{66,2},{3,67},{67,3},{4,68},{68... | collective-permute-start | bytes 428 | tf_op jit(solution)/shard_map/ppermute | solution.py:397
  68.4 1.3 copy-start
  70.5 7.7 %collective-permute-start.6 = (f32[16,16,128]{2,1,0:T(8,128)}, f32[16,16,128]{2,1,0:T(8,128)S(1)}, u32[]{:S(2)}, u32[]{:S(2)}) collective-permute-start(f32[16,16,128]{2,1,0:T(8,128)} %get-tuple-element.43), channel_id=1, source_target_pairs={{64,0},{2,1},{66,2},{4,3},{68,4},{6,5},{70,6},{65,64},{1,65},{67,6... | collective-permute-start | bytes 393224 | tf_op jit(solution)/shard_map/ppermute | solution.py:415
  72.4 6.7 %collective-permute-start.5 = (f32[16,16,128]{2,1,0:T(8,128)}, f32[16,16,128]{2,1,0:T(8,128)S(1)}, u32[]{:S(2)}, u32[]{:S(2)}) collective-permute-start(f32[16,16,128]{2,1,0:T(8,128)} %get-tuple-element.44), channel_id=1, source_target_pairs={{0,64},{1,2},{2,66},{3,4},{4,68},{5,6},{6,70},{64,65},{65,1},{66,6... | collective-permute-start | bytes 393224 | tf_op jit(solution)/shard_map/ppermute | solution.py:414
  76.6 0.6 copy-start.1
  77.2 0.6 copy-start.4
  85.3 0.8 copy-start.2
  86.1 0.8 copy-start.5
  86.9 40.1 %copy-start.3 = (bf16[128,256]{1,0:T(8,128)(2,1)S(1)}, bf16[128,256]{1,0:T(8,128)(2,1)}, u32[]{:S(2)}) copy-start(bf16[128,256]{1,0:T(8,128)(2,1)} %copy-done.1) | copy-start | bytes 196612
  109.0 11.2 %collective-permute-start.9 = (f32[6,136,128]{2,1,0:T(8,128)S(1)}, f32[6,136,128]{2,1,0:T(8,128)S(1)}, u32[]{:S(2)}, u32[]{:S(2)}) collective-permute-start(f32[6,136,128]{2,1,0:T(8,128)S(1)} %get-tuple-element.36), channel_id=1, source_target_pairs={{0,8},{8,16},{16,24},{24,32},{32,40},{40,48},{48,56},{1,9},{9,17},... | collective-permute-start | bytes 1253384 | tf_op jit(solution)/shard_map/ppermute | solution.py:431
  110.9 16.1 %collective-permute-start.10 = (f32[6,136,128]{2,1,0:T(8,128)S(1)}, f32[6,136,128]{2,1,0:T(8,128)S(1)}, u32[]{:S(2)}, u32[]{:S(2)}) collective-permute-start(f32[6,136,128]{2,1,0:T(8,128)S(1)} %get-tuple-element.38), channel_id=1, source_target_pairs={{8,0},{16,8},{24,16},{32,24},{40,32},{48,40},{56,48},{9,1},{17,9},... | collective-permute-start | bytes 1253384 | tf_op jit(solution)/shard_map/ppermute | solution.py:431
  134.4 39.0 %collective-permute-start.12 = (f32[2,64,8,128]{3,2,1,0:T(8,128)S(1)}, f32[2,64,8,128]{3,2,1,0:T(8,128)S(1)}, u32[]{:S(2)}, u32[]{:S(2)}) collective-permute-start(f32[2,64,8,128]{3,2,1,0:T(8,128)S(1)} %iterate.7.refs_0_), channel_id=1, source_target_pairs={{0,64},{64,0},{1,65},{65,1},{2,66},{66,2},{3,67},{67,3},{4,68},{68... | collective-permute-start | bytes 1572872 | tf_op jit(solution)/shard_map/ppermute | solution.py:438
  142.5 30.1 %collective-permute-start.13 = (f32[2,64,8,128]{3,2,1,0:T(8,128)S(1)}, f32[2,64,8,128]{3,2,1,0:T(8,128)S(1)}, u32[]{:S(2)}, u32[]{:S(2)}) collective-permute-start(f32[2,64,8,128]{3,2,1,0:T(8,128)S(1)} %iterate.8.refs_0_), channel_id=1, source_target_pairs={{0,64},{64,0},{1,65},{65,1},{2,66},{66,2},{3,67},{67,3},{4,68},{68... | collective-permute-start | bytes 1572872 | tf_op jit(solution)/shard_map/ppermute | solution.py:438
  152.6 19.3 %collective-permute-start.14 = (f32[2,64,8,128]{3,2,1,0:T(8,128)S(1)}, f32[2,64,8,128]{3,2,1,0:T(8,128)S(1)}, u32[]{:S(2)}, u32[]{:S(2)}) collective-permute-start(f32[2,64,8,128]{3,2,1,0:T(8,128)S(1)} %iterate.9.refs_0_), channel_id=1, source_target_pairs={{0,64},{64,0},{1,65},{65,1},{2,66},{66,2},{3,67},{67,3},{4,68},{68... | collective-permute-start | bytes 1572872 | tf_op jit(solution)/shard_map/ppermute | solution.py:438
  160.8 19.4 %collective-permute-start.11 = (f32[2,64,8,128]{3,2,1,0:T(8,128)S(1)}, f32[2,64,8,128]{3,2,1,0:T(8,128)S(1)}, u32[]{:S(2)}, u32[]{:S(2)}) collective-permute-start(f32[2,64,8,128]{3,2,1,0:T(8,128)S(1)} %iterate.6.refs_0_), channel_id=1, source_target_pairs={{0,64},{64,0},{1,65},{65,1},{2,66},{66,2},{3,67},{67,3},{4,68},{68... | collective-permute-start | bytes 1572872 | tf_op jit(solution)/shard_map/ppermute | solution.py:438

commit v3 on v2

--- a/solution.py
+++ b/solution.py
@@ -19,12 +19,12 @@
 GROUP = 8
 EXT_R = ROWS + 2 * PAD
 EXT_C = HALF + 2 * MARGIN
-VMEM_BYTES = 48 * 1024 * 1024
+MIB = 1024 * 1024
 TINY = 1e-30
 
 
-def params(**kwargs):
-    return pltpu.CompilerParams(vmem_limit_bytes=VMEM_BYTES, **kwargs)
+def params(mib):
+    return pltpu.CompilerParams(vmem_limit_bytes=mib * MIB)
 
 
 def blocks_of(total, largest=96):
@@ -65,7 +65,7 @@
             jax.ShapeDtypeStruct((2 * Z, 2 * LANES), jnp.bfloat16),
             jax.ShapeDtypeStruct((2 * LANES, LANES), jnp.bfloat16),
         ),
-        compiler_params=params(),
+        compiler_params=params(4),
         name="matrices",
     )(kz)
 
@@ -84,12 +84,13 @@
 
 
 def turn(where, recorded, received, first_group, group_step):
+    count = received.shape[1] // GROUP
     return pl.pallas_call(
         turn_kernel,
-        out_shape=jax.ShapeDtypeStruct((2 * GROUP, HALF, LANES), jnp.float32),
+        out_shape=jax.ShapeDtypeStruct((count * GROUP, HALF, LANES), jnp.float32),
         grid_spec=pltpu.PrefetchScalarGridSpec(
             num_scalar_prefetch=1,
-            grid=(2, 2),
+            grid=(count, 2),
             in_specs=[
                 pl.BlockSpec(
                     (1, Z, GROUP, CHUNK),
@@ -99,25 +100,27 @@
             ],
             out_specs=pl.BlockSpec((GROUP, CHUNK, LANES), lambda i, j, w: (i, j, 0)),
         ),
-        cost_estimate=pl.CostEstimate(flops=0, bytes_accessed=4 << 20, transcendentals=0),
-        compiler_params=params(),
+        cost_estimate=pl.CostEstimate(
+            flops=0, bytes_accessed=count << 21, transcendentals=0
+        ),
+        compiler_params=params(8),
         name="turn",
     )(where, recorded, received)
 
 
 SPANS = ((0, PAD),) + tuple((PAD + GROUP * g, GROUP) for g in range(4)) + ((EXT_R - PAD, PAD),)
-HOMES = ((0, 0), (1, 0), (1, GROUP), (0, GROUP))
-
-
-def iterate_kernel(first, row0, n_out, *refs):
+HOMES = ((0, 0), (1, 0), (2, 0), (0, GROUP))
+
+
+def iterate_kernel(first, row0, n_out, present, *refs):
     n_in = n_out + 2 * PAD
     width = EXT_C if first else EXT_C - 2 * SIDE
     shift = 0 if first else SIDE
     inner = width - 2 * SIDE
     fold = (EXT_C - 2 * SIDE) // 2
-    recorded, refs = refs[:8], refs[8:]
-    if not first:
-        field, refs = refs[:3], refs[3:]
+    pieces = iter(refs)
+    taken = [next(pieces) if there else None for there in present]
+    recorded, field, refs = taken[:11], taken[11:], tuple(pieces)
     taps_ref, blur_ref, adj_ref = refs[:3]
     refs = refs[3:]
     if first:
@@ -126,7 +129,7 @@
     else:
         out_ref, refs = refs[0], refs[1:]
     r_buf, e_buf, xz_buf, xr_buf, pack, tmp, r_sem, e_sem = refs
-    north, south = recorded[0], recorded[7]
+    north, south = recorded[0], recorded[10]
     lower = lax.broadcasted_iota(jnp.int32, (width, LANES), 1) < Z
 
     def window(span, lo, hi):
@@ -296,19 +299,24 @@
     n_in = n_out + 2 * PAD
     width = EXT_C if first else EXT_C - 2 * SIDE
     fold = (EXT_C - 2 * SIDE) // 2
+    pieces = list(recorded) + (list(field) if field is not None else [])
+    if not first and row0 >= PAD:
+        pieces[0] = pieces[11] = None
+    if not first and row0 + n_in <= EXT_R - PAD:
+        pieces[10] = pieces[13] = None
+    present = tuple(piece is not None for piece in pieces)
+    pieces = [piece for piece in pieces if piece is not None]
     if first:
         edge = jax.ShapeDtypeStruct((PAD, fold, LANES), jnp.float32)
         out = (jax.ShapeDtypeStruct((ROWS, EXT_C - 2 * SIDE, LANES), jnp.float32), edge, edge)
         out_specs = (pl.BlockSpec(memory_space=pltpu.VMEM),) * 3
-        pieces = list(recorded)
     else:
         out = jax.ShapeDtypeStruct((2, Z, GROUP, CHUNK), jnp.float32)
         out_specs = pl.BlockSpec(memory_space=pltpu.VMEM)
-        pieces = list(recorded) + list(field)
     row = pltpu.VMEM((n_in, width, LANES), jnp.float32)
     vregs = n_in * width // 8
     return pl.pallas_call(
-        functools.partial(iterate_kernel, first, row0, n_out),
+        functools.partial(iterate_kernel, first, row0, n_out, present),
         out_shape=out,
         in_specs=[pl.BlockSpec(memory_space=pl.ANY)] * len(pieces)
         + [pl.BlockSpec(memory_space=pltpu.VMEM)] * 3,
@@ -326,7 +334,7 @@
         cost_estimate=pl.CostEstimate(
             flops=vregs * 1024 * 70, bytes_accessed=vregs * 4096 * 3, transcendentals=0
         ),
-        compiler_params=params(),
+        compiler_params=params(36 if first else 16),
         name="iterate",
     )(*pieces, taps, blur, adj)
 
@@ -354,7 +362,7 @@
         ),
         input_output_aliases=aliases,
         cost_estimate=pl.CostEstimate(flops=0, bytes_accessed=1 << 20, transcendentals=0),
-        compiler_params=params(),
+        compiler_params=params(4),
         name="place",
     )(*args)
 
@@ -390,11 +398,16 @@
         )
 
     border_in = lax.ppermute(other_rows((0, GROUP), (ROWS - GROUP, GROUP)), "view", swap)
-    inner_in = lax.ppermute(other_rows((GROUP, 2 * GROUP)), "view", swap)
-
-    norm = lambda k: k[0] / jnp.sum(k[0])
-    own = jnp.concatenate([norm(psf_axial), norm(psf_rows), norm(psf_cols)])
-    other = lax.ppermute(own, "view", swap)
+    raw = jnp.concatenate([psf_axial[0], psf_rows[0], psf_cols[0]])
+    raw_other = lax.ppermute(raw, "view", swap)
+    upper, raw_other = lax.optimization_barrier((other_rows((GROUP, GROUP)), raw_other))
+    upper_in = lax.ppermute(upper, "view", swap)
+
+    def norm(taps):
+        parts = (taps[:21], taps[21:28], taps[28:35])
+        return jnp.concatenate([part / jnp.sum(part) for part in parts])
+
+    own, other = norm(raw), norm(raw_other)
     view = lax.axis_index("view")
     lanes = jnp.concatenate(
         [
@@ -416,14 +429,17 @@
         return west, block, east
 
     border = widen(turn(where, views_data, border_in, 0, 3))
+    lower, border = lax.optimization_barrier((other_rows((2 * GROUP, GROUP)), border))
+    lower_in = lax.ppermute(lower, "view", swap)
 
     def edge(rows):
         return jnp.concatenate([part[rows] for part in border], axis=1)
 
     north = lax.ppermute(edge(slice(2 * GROUP - PAD, 2 * GROUP)), "ty", down)
     south = lax.ppermute(edge(slice(0, PAD)), "ty", up)
-    inner = widen(turn(where, views_data, inner_in, 1, 1))
-    recorded = (north,) + border + inner + (south,)
+    upper = widen(turn(where, views_data, upper_in, 1, 1))
+    lower = widen(turn(where, views_data, lower_in, 2, 1))
+    recorded = (north,) + border + upper + lower + (south,)
 
     estimate, top, low = iterate(
         recorded, None, taps, blur, adj, first=True, row0=0, n_out=ROWS

time: 182 us -> 174 us (0.956)
  the two profiles are of different devices: /device:TPU:26 before, /device:TPU:90 now
where the time goes in v3:
time: 174 us; the launch traced here: 173 us
  Pallas kernels  62 us (36%)
  waiting for transfers between devices  51.2 us (29%)
  starting transfers between devices  39.4 us (23%)
  local copies, waits for them, and re-layouts  10.2 us (6%)
  other arithmetic  10.2 us (6%)
    pallas_call x5, Pallas kernels, iterate(): pl.pallas_call(functools.partial(iterate_kernel, first, row0, n_out, pres...  51 us
    ppermute x1, waiting for transfers between devices, per_device(): raw_other = lax.ppermute(raw, 'view', swap)  18.4 us
    ppermute x1, waiting for transfers between devices, per_device(): lower_in = lax.ppermute(lower, 'view', swap)  15.9 us
    ppermute x4, waiting for transfers between devices, per_device(): theirs.append((group, lax.ppermute(block, 'view', swap)))  12.9 us
    ppermute x3, starting transfers between devices, widen(): west = lax.ppermute(block[:, HALF - MARGIN:], ('view', 'tx'), right)  11.8 us
    pallas_call x8, Pallas kernels, place(): pl.pallas_call(place_kernel, out_shape=jax.ShapeDtypeStruct((Z, ROWS, 2 *...  6.46 us
    ppermute x3, starting transfers between devices, widen(): east = lax.ppermute(block[:, :MARGIN], ('view', 'tx'), left)  6 us
    unnamed x20, local copies, waits for them, and re-layouts  5.87 us
  transfers between devices with their start and end apart: 18, of which 7 were waited for; matrix products, arithmetic and copies ran while one was open for 7% of the time, Pallas kernels for 23%

profile of v3, /device:TPU:90, one launch (start us, length us, event | category | flops | bytes accessed | tf_op | source)
XLA Modules:
  0.0 173.3 jit_solution(14046815551299626183)
XLA Ops:
  0.0 2.6 %dynamic-slice_bitcast_fusion = (f32[64,8,256]{2,1,0:T(8,128)}, f32[64,8,256]{2,1,0:T(8,128)S(1)}, f32[64,8,256]{2,1,0:T(8,128)S(1)}, f32[64,8,256]{2,1,0:T(8,128)}) fusion(f32[1,64,32,512]{3,2,1,0:T(8,128)} %own_ref.5, s32[]{:T(128)S(6)} %select_n.26), kind=kLoop, calls=%fused_computation.3 | loop fusion | bytes 4194308 | tf_op jit(solution)/shard_map/squeeze | solution.py:394
  2.8 1.7 collective-permute-start
  8.0 1.3 broadcast_divide_fusion
  9.4 18.4 %collective-permute-done.3 = f32[35]{0:T(128)S(1)} collective-permute-done((f32[35]{0:T(128)S(1)}, f32[35]{0:T(128)S(1)}, u32[]{:S(2)}, u32[]{:S(2)}) %collective-permute-start.3) | collective-permute-done | bytes 172 | tf_op jit(solution)/shard_map/ppermute | solution.py:402
  27.8 1.6 collective-permute-start.4
  30.8 1.4 slice_divide_fusion.1
  32.2 2.2 %copy-done = f32[1,64,32,512]{3,2,1,0:T(8,128)S(1)} copy-done((f32[1,64,32,512]{3,2,1,0:T(8,128)S(1)}, f32[1,64,32,512]{3,2,1,0:T(8,128)}, u32[]{:S(2)}) %copy-start) | copy-done | bytes 4194328
  34.4 1.9 %turn.3.refs_2_.refs_1_ = f32[16,256,128]{2,1,0:T(8,128)S(1)} custom-call(s32[2]{0:T(128)S(1)} %pad_add_fusion.where_ref, f32[1,64,32,512]{3,2,1,0:T(8,128)S(1)} %copy-done, f32[64,16,256]{2,1,0:T(8,128)S(1)} %collective-permute-done.other_ref), custom_call_target="tpu_custom_call" | custom-call | bytes 4194304 | tf_op jit(solution)/shard_map/turn/pallas_call | solution.py:88
  36.4 2.2 %collective-permute-start.2 = (f32[16,16,128]{2,1,0:T(8,128)S(1)}, f32[16,16,128]{2,1,0:T(8,128)S(1)}, u32[]{:S(2)}, u32[]{:S(2)}) collective-permute-start(f32[16,16,128]{2,1,0:T(8,128)S(1)} %get-tuple-element.59), channel_id=1, source_target_pairs={{64,0},{2,1},{66,2},{4,3},{68,4},{6,5},{70,6},{65,64},{1,65},{67,6... | collective-permute-start | bytes 393224 | tf_op jit(solution)/shard_map/ppermute | solution.py:428
  38.5 3.9 %collective-permute-start.1 = (f32[16,16,128]{2,1,0:T(8,128)S(1)}, f32[16,16,128]{2,1,0:T(8,128)S(1)}, u32[]{:S(2)}, u32[]{:S(2)}) collective-permute-start(f32[16,16,128]{2,1,0:T(8,128)S(1)} %get-tuple-element.60), channel_id=1, source_target_pairs={{0,64},{1,2},{2,66},{3,4},{4,68},{5,6},{6,70},{64,65},{65,1},{66,6... | collective-permute-start | bytes 393224 | tf_op jit(solution)/shard_map/ppermute | solution.py:427
  43.1 1.7 collective-permute-done.2.refs_3_.refs_2_
  45.0 2.4 %collective-permute-start.7 = (f32[64,8,256]{2,1,0:T(8,128)}, f32[64,8,256]{2,1,0:T(8,128)S(1)}, u32[]{:S(2)}, u32[]{:S(2)}) collective-permute-start(f32[64,8,256]{2,1,0:T(8,128)} %get-tuple-element.44), channel_id=1, source_target_pairs={{0,64},{64,0},{1,65},{65,1},{2,66},{66,2},{3,67},{67,3},{4,68},{68... | collective-permute-start | bytes 1572872 | tf_op jit(solution)/shard_map/ppermute | solution.py:433
  48.6 3.6 %collective-permute-start.10 = (f32[6,288,128]{2,1,0:T(8,128)}, f32[6,288,128]{2,1,0:T(8,128)}, u32[]{:S(2)}, u32[]{:S(2)}) collective-permute-start(f32[6,288,128]{2,1,0:T(8,128)} %pad_maximum_fusion.1), channel_id=1, source_target_pairs={{8,0},{16,8},{24,16},{32,24},{40,32},{48,40},{56,48},{9,1},{17,9},... | collective-permute-start | bytes 2654216 | tf_op jit(solution)/shard_map/ppermute | solution.py:439
  53.1 1.3 collective-permute-start.11
  56.9 1.9 %collective-permute-start.6 = (f32[8,16,128]{2,1,0:T(8,128)S(1)}, f32[8,16,128]{2,1,0:T(8,128)S(1)}, u32[]{:S(2)}, u32[]{:S(2)}) collective-permute-start(f32[8,16,128]{2,1,0:T(8,128)S(1)} %get-tuple-element.63), channel_id=1, source_target_pairs={{64,0},{2,1},{66,2},{4,3},{68,4},{6,5},{70,6},{65,64},{1,65},{67,6... | collective-permute-start | bytes 196616 | tf_op jit(solution)/shard_map/ppermute | solution.py:428
  58.8 3.9 %collective-permute-start.5 = (f32[8,16,128]{2,1,0:T(8,128)}, f32[8,16,128]{2,1,0:T(8,128)}, u32[]{:S(2)}, u32[]{:S(2)}) collective-permute-start(f32[8,16,128]{2,1,0:T(8,128)} %get-tuple-element.64), channel_id=1, source_target_pairs={{0,64},{1,2},{2,66},{3,4},{4,68},{5,6},{6,70},{64,65},{65,1},{66,6... | collective-permute-start | bytes 196616 | tf_op jit(solution)/shard_map/ppermute | solution.py:427
  62.7 15.9 %collective-permute-done.7.other_ref = f32[64,8,256]{2,1,0:T(8,128)S(1)} collective-permute-done((f32[64,8,256]{2,1,0:T(8,128)}, f32[64,8,256]{2,1,0:T(8,128)S(1)}, u32[]{:S(2)}, u32[]{:S(2)}) %collective-permute-start.7) | collective-permute-done | bytes 524320 | tf_op jit(solution)/shard_map/ppermute | solution.py:433
  81.5 1.9 %collective-permute-start.9 = (f32[8,16,128]{2,1,0:T(8,128)}, f32[8,16,128]{2,1,0:T(8,128)}, u32[]{:S(2)}, u32[]{:S(2)}) collective-permute-start(f32[8,16,128]{2,1,0:T(8,128)} %get-tuple-element.61), channel_id=1, source_target_pairs={{64,0},{2,1},{66,2},{4,3},{68,4},{6,5},{70,6},{65,64},{1,65},{67,6... | collective-permute-start | bytes 196616 | tf_op jit(solution)/shard_map/ppermute | solution.py:428
  84.1 3.9 %collective-permute-start.8 = (f32[8,16,128]{2,1,0:T(8,128)}, f32[8,16,128]{2,1,0:T(8,128)}, u32[]{:S(2)}, u32[]{:S(2)}) collective-permute-start(f32[8,16,128]{2,1,0:T(8,128)} %get-tuple-element.62), channel_id=1, source_target_pairs={{0,64},{1,2},{2,66},{3,4},{4,68},{5,6},{6,70},{64,65},{65,1},{66,6... | collective-permute-start | bytes 196616 | tf_op jit(solution)/shard_map/ppermute | solution.py:427
  88.2 2.0 %collective-permute-done.8.refs_7_.refs_6_ = f32[8,16,128]{2,1,0:T(8,128)} collective-permute-done((f32[8,16,128]{2,1,0:T(8,128)}, f32[8,16,128]{2,1,0:T(8,128)}, u32[]{:S(2)}, u32[]{:S(2)}) %collective-permute-start.8) | collective-permute-done | bytes 65568 | tf_op jit(solution)/shard_map/ppermute | solution.py:427
  90.2 1.2 copy-done.3
  92.3 20.8 %iterate.5 = (f32[32,272,128]{2,1,0:T(8,128)S(1)}, f32[6,136,128]{2,1,0:T(8,128)S(1)}, f32[6,136,128]{2,1,0:T(8,128)S(1)}) custom-call(f32[6,288,128]{2,1,0:T(8,128)} %collective-permute-done.11.refs_0_, f32[16,16,128]{2,1,0:T(8,128)S(1)} %collective-permute-done.1.refs_1_.refs_0_, f32[16,256,128]{2,1,0:T(8,128)S(1)} %turn.3.refs_2_.refs_1_, ...), custom_call_target="tpu_custom_call" | custom-call | flops 113541120 | bytes 19464192 | tf_op jit(solution)/shard_map/iterate/pallas_call | solution.py:318
  113.1 1.3 collective-permute-start.14
  114.4 4.6 %collective-permute-start.12 = (f32[6,136,128]{2,1,0:T(8,128)S(1)}, f32[6,136,128]{2,1,0:T(8,128)S(1)}, u32[]{:S(2)}, u32[]{:S(2)}) collective-permute-start(f32[6,136,128]{2,1,0:T(8,128)S(1)} %get-tuple-element.49), channel_id=1, source_target_pairs={{8,0},{16,8},{24,16},{32,24},{40,32},{48,40},{56,48},{9,1},{17,9},... | collective-permute-start | bytes 1253384 | tf_op jit(solution)/shard_map/ppermute | solution.py:447
  119.0 7.4 %iterate.8.refs_0_ = f32[2,64,8,128]{3,2,1,0:T(8,128)S(1)} custom-call(f32[16,16,128]{2,1,0:T(8,128)S(1)} %collective-permute-done.1.refs_1_.refs_0_, f32[16,256,128]{2,1,0:T(8,128)S(1)} %turn.3.refs_2_.refs_1_, f32[16,16,128]{2,1,0:T(8,128)S(1)} %collective-permute-done.2.refs_3_.refs_2_, f32[8,16,128]{2,1,0:T(8,128)} %collective-permute-done.5.refs_4_.refs_3_, ...), custom_call_target="tpu_custom_call" | custom-call | flops 48742400 | bytes 8355840 | tf_op jit(solution)/shard_map/iterate/pallas_call | solution.py:318
  126.4 2.4 %collective-permute-start.16 = (f32[2,64,8,128]{3,2,1,0:T(8,128)S(1)}, f32[2,64,8,128]{3,2,1,0:T(8,128)S(1)}, u32[]{:S(2)}, u32[]{:S(2)}) collective-permute-start(f32[2,64,8,128]{3,2,1,0:T(8,128)S(1)} %iterate.8.refs_0_), channel_id=1, source_target_pairs={{0,64},{64,0},{1,65},{65,1},{2,66},{66,2},{3,67},{67,3},{4,68},{68... | collective-permute-start | bytes 1572872 | tf_op jit(solution)/shard_map/ppermute | solution.py:454
  128.8 7.4 %iterate.9.refs_0_ = f32[2,64,8,128]{3,2,1,0:T(8,128)S(1)} custom-call(f32[16,16,128]{2,1,0:T(8,128)S(1)} %collective-permute-done.1.refs_1_.refs_0_, f32[16,256,128]{2,1,0:T(8,128)S(1)} %turn.3.refs_2_.refs_1_, f32[16,16,128]{2,1,0:T(8,128)S(1)} %collective-permute-done.2.refs_3_.refs_2_, f32[8,16,128]{2,1,0:T(8,128)} %collective-permute-done.5.refs_4_.refs_3_, ...), custom_call_target="tpu_custom_call" | custom-call | flops 48742400 | bytes 8355840 | tf_op jit(solution)/shard_map/iterate/pallas_call | solution.py:318
  136.4 7.7 %iterate.7.refs_0_ = f32[2,64,8,128]{3,2,1,0:T(8,128)S(1)} custom-call(f32[6,288,128]{2,1,0:T(8,128)} %collective-permute-done.11.refs_0_, f32[16,16,128]{2,1,0:T(8,128)S(1)} %collective-permute-done.1.refs_1_.refs_0_, f32[16,256,128]{2,1,0:T(8,128)S(1)} %turn.3.refs_2_.refs_1_, f32[16,16,128]{2,1,0:T(8,128)S(1)} %collective-permute-done.2.refs_3_.refs_2_, ...), custom_call_target="tpu_custom_call" | custom-call | flops 48742400 | bytes 8355840 | tf_op jit(solution)/shard_map/iterate/pallas_call | solution.py:318
  144.0 2.1 %collective-permute-start.15 = (f32[2,64,8,128]{3,2,1,0:T(8,128)S(1)}, f32[2,64,8,128]{3,2,1,0:T(8,128)S(1)}, u32[]{:S(2)}, u32[]{:S(2)}) collective-permute-start(f32[2,64,8,128]{3,2,1,0:T(8,128)S(1)} %iterate.7.refs_0_), channel_id=1, source_target_pairs={{0,64},{64,0},{1,65},{65,1},{2,66},{66,2},{3,67},{67,3},{4,68},{68... | collective-permute-start | bytes 1572872 | tf_op jit(solution)/shard_map/ppermute | solution.py:454
  146.1 7.6 %iterate.6.refs_0_ = f32[2,64,8,128]{3,2,1,0:T(8,128)S(1)} custom-call(f32[16,16,128]{2,1,0:T(8,128)S(1)} %collective-permute-done.1.refs_1_.refs_0_, f32[16,256,128]{2,1,0:T(8,128)S(1)} %turn.3.refs_2_.refs_1_, f32[16,16,128]{2,1,0:T(8,128)S(1)} %collective-permute-done.2.refs_3_.refs_2_, f32[8,16,128]{2,1,0:T(8,128)} %collective-permute-done.5.refs_4_.refs_3_, ...), custom_call_target="tpu_custom_call" | custom-call | flops 48742400 | bytes 8355840 | tf_op jit(solution)/shard_map/iterate/pallas_call | solution.py:318
  158.8 5.4 %collective-permute-done.15.refs_0_ = f32[2,64,8,128]{3,2,1,0:T(8,128)S(1)} collective-permute-done((f32[2,64,8,128]{3,2,1,0:T(8,128)S(1)}, f32[2,64,8,128]{3,2,1,0:T(8,128)S(1)}, u32[]{:S(2)}, u32[]{:S(2)}) %collective-permute-start.15) | collective-permute-done | bytes 524320 | tf_op jit(solution)/shard_map/ppermute | solution.py:454
  165.0 7.5 %collective-permute-done.13.refs_0_ = f32[2,64,8,128]{3,2,1,0:T(8,128)S(1)} collective-permute-done((f32[2,64,8,128]{3,2,1,0:T(8,128)S(1)}, f32[2,64,8,128]{3,2,1,0:T(8,128)S(1)}, u32[]{:S(2)}, u32[]{:S(2)}) %collective-permute-start.13) | collective-permute-done | bytes 524320 | tf_op jit(solution)/shard_map/ppermute | solution.py:454
  (68 shorter events, 21.6 us)
Async XLA Ops:
  0.0 4.5 %copy-start.9 = (f32[1,21]{1,0:T(1,128)S(1)}, f32[1,21]{1,0:T(1,128)}, u32[]{:S(2)}) copy-start(f32[1,21]{1,0:T(1,128)} %param.9) | copy-start | bytes 256
  0.0 4.5 %copy-start.7 = (f32[1,7]{1,0:T(1,128)S(1)}, f32[1,7]{1,0:T(1,128)}, u32[]{:S(2)}) copy-start(f32[1,7]{1,0:T(1,128)} %param.10) | copy-start | bytes 88
  0.0 4.5 %copy-start.6 = (f32[1,7]{1,0:T(1,128)S(1)}, f32[1,7]{1,0:T(1,128)}, u32[]{:S(2)}) copy-start(f32[1,7]{1,0:T(1,128)} %param.11) | copy-start | bytes 88
  2.8 29.4 %collective-permute-start = (f32[64,16,256]{2,1,0:T(8,128)S(1)}, f32[64,16,256]{2,1,0:T(8,128)S(1)}, u32[]{:S(2)}, u32[]{:S(2)}) collective-permute-start(f32[64,16,256]{2,1,0:T(8,128)S(1)} %pad_maximum_fusion), channel_id=1, source_target_pairs={{0,64},{64,0},{1,65},{65,1},{2,66},{66,2},{3,67},{67,3},{4,68},{68... | collective-permute-start | bytes 3145736 | tf_op jit(solution)/shard_map/ppermute | solution.py:400
  4.5 23.3 %collective-permute-start.3 = (f32[35]{0:T(128)S(1)}, f32[35]{0:T(128)S(1)}, u32[]{:S(2)}, u32[]{:S(2)}) collective-permute-start(f32[35]{0:T(128)S(1)} %pad_maximum_fusion.5), channel_id=1, source_target_pairs={{0,64},{64,0},{1,65},{65,1},{2,66},{66,2},{3,67},{67,3},{4,68},{68... | collective-permute-start | bytes 428 | tf_op jit(solution)/shard_map/ppermute | solution.py:402
  27.8 27.2 %collective-permute-start.4 = (f32[64,8,256]{2,1,0:T(8,128)}, f32[64,8,256]{2,1,0:T(8,128)S(1)}, u32[]{:S(2)}, u32[]{:S(2)}) collective-permute-start(f32[64,8,256]{2,1,0:T(8,128)} %get-tuple-element.43), channel_id=1, source_target_pairs={{0,64},{64,0},{1,65},{65,1},{2,66},{66,2},{3,67},{67,3},{4,68},{68... | collective-permute-start | bytes 1572872 | tf_op jit(solution)/shard_map/ppermute | solution.py:404
  32.2 2.2 %copy-start = (f32[1,64,32,512]{3,2,1,0:T(8,128)S(1)}, f32[1,64,32,512]{3,2,1,0:T(8,128)}, u32[]{:S(2)}) copy-start(f32[1,64,32,512]{3,2,1,0:T(8,128)} %own_ref.5) | copy-start | bytes 12582916
  36.3 18.1 %copy-start.8 = (f32[21]{0:T(128)S(1)}, f32[21]{0:T(128)}, u32[]{:S(2)}) copy-start(f32[21]{0:T(128)} %broadcast_divide_fusion.2) | copy-start | bytes 256
  36.3 18.7 %copy-start.1 = (f32[1,64,32,512]{3,2,1,0:T(8,128)S(1)}, f32[1,64,32,512]{3,2,1,0:T(8,128)}, u32[]{:S(2)}) copy-start(f32[1,64,32,512]{3,2,1,0:T(8,128)} %own_ref.5) | copy-start | bytes 12582916
  36.4 8.4 %collective-permute-start.2 = (f32[16,16,128]{2,1,0:T(8,128)S(1)}, f32[16,16,128]{2,1,0:T(8,128)S(1)}, u32[]{:S(2)}, u32[]{:S(2)}) collective-permute-start(f32[16,16,128]{2,1,0:T(8,128)S(1)} %get-tuple-element.59), channel_id=1, source_target_pairs={{64,0},{2,1},{66,2},{4,3},{68,4},{6,5},{70,6},{65,64},{1,65},{67,6... | collective-permute-start | bytes 393224 | tf_op jit(solution)/shard_map/ppermute | solution.py:428
  38.5 6.4 %collective-permute-start.1 = (f32[16,16,128]{2,1,0:T(8,128)S(1)}, f32[16,16,128]{2,1,0:T(8,128)S(1)}, u32[]{:S(2)}, u32[]{:S(2)}) collective-permute-start(f32[16,16,128]{2,1,0:T(8,128)S(1)} %get-tuple-element.60), channel_id=1, source_target_pairs={{0,64},{1,2},{2,66},{3,4},{4,68},{5,6},{6,70},{64,65},{65,1},{66,6... | collective-permute-start | bytes 393224 | tf_op jit(solution)/shard_map/ppermute | solution.py:427
  45.0 33.7 %collective-permute-start.7 = (f32[64,8,256]{2,1,0:T(8,128)}, f32[64,8,256]{2,1,0:T(8,128)S(1)}, u32[]{:S(2)}, u32[]{:S(2)}) collective-permute-start(f32[64,8,256]{2,1,0:T(8,128)} %get-tuple-element.44), channel_id=1, source_target_pairs={{0,64},{64,0},{1,65},{65,1},{2,66},{66,2},{3,67},{67,3},{4,68},{68... | collective-permute-start | bytes 1572872 | tf_op jit(solution)/shard_map/ppermute | solution.py:433
  48.6 41.6 %collective-permute-start.10 = (f32[6,288,128]{2,1,0:T(8,128)}, f32[6,288,128]{2,1,0:T(8,128)}, u32[]{:S(2)}, u32[]{:S(2)}) collective-permute-start(f32[6,288,128]{2,1,0:T(8,128)} %pad_maximum_fusion.1), channel_id=1, source_target_pairs={{8,0},{16,8},{24,16},{32,24},{40,32},{48,40},{56,48},{9,1},{17,9},... | collective-permute-start | bytes 2654216 | tf_op jit(solution)/shard_map/ppermute | solution.py:439
  53.1 37.1 %collective-permute-start.11 = (f32[6,288,128]{2,1,0:T(8,128)}, f32[6,288,128]{2,1,0:T(8,128)}, u32[]{:S(2)}, u32[]{:S(2)}) collective-permute-start(f32[6,288,128]{2,1,0:T(8,128)} %pad_maximum_fusion.2), channel_id=1, source_target_pairs={{0,8},{8,16},{16,24},{24,32},{32,40},{40,48},{48,56},{1,9},{9,17},... | collective-permute-start | bytes 2654216 | tf_op jit(solution)/shard_map/ppermute | solution.py:438
  56.9 26.6 %collective-permute-start.6 = (f32[8,16,128]{2,1,0:T(8,128)S(1)}, f32[8,16,128]{2,1,0:T(8,128)S(1)}, u32[]{:S(2)}, u32[]{:S(2)}) collective-permute-start(f32[8,16,128]{2,1,0:T(8,128)S(1)} %get-tuple-element.63), channel_id=1, source_target_pairs={{64,0},{2,1},{66,2},{4,3},{68,4},{6,5},{70,6},{65,64},{1,65},{67,6... | collective-permute-start | bytes 196616 | tf_op jit(solution)/shard_map/ppermute | solution.py:428
  58.8 29.4 %collective-permute-start.5 = (f32[8,16,128]{2,1,0:T(8,128)}, f32[8,16,128]{2,1,0:T(8,128)}, u32[]{:S(2)}, u32[]{:S(2)}) collective-permute-start(f32[8,16,128]{2,1,0:T(8,128)} %get-tuple-element.64), channel_id=1, source_target_pairs={{0,64},{1,2},{2,66},{3,4},{4,68},{5,6},{6,70},{64,65},{65,1},{66,6... | collective-permute-start | bytes 196616 | tf_op jit(solution)/shard_map/ppermute | solution.py:427
  80.5 1.0 copy-start.2
  81.5 6.6 %collective-permute-start.9 = (f32[8,16,128]{2,1,0:T(8,128)}, f32[8,16,128]{2,1,0:T(8,128)}, u32[]{:S(2)}, u32[]{:S(2)}) collective-permute-start(f32[8,16,128]{2,1,0:T(8,128)} %get-tuple-element.61), channel_id=1, source_target_pairs={{64,0},{2,1},{66,2},{4,3},{68,4},{6,5},{70,6},{65,64},{1,65},{67,6... | collective-permute-start | bytes 196616 | tf_op jit(solution)/shard_map/ppermute | solution.py:428
  83.4 0.6 copy-start.4
  84.1 6.1 %collective-permute-start.8 = (f32[8,16,128]{2,1,0:T(8,128)}, f32[8,16,128]{2,1,0:T(8,128)}, u32[]{:S(2)}, u32[]{:S(2)}) collective-permute-start(f32[8,16,128]{2,1,0:T(8,128)} %get-tuple-element.62), channel_id=1, source_target_pairs={{0,64},{1,2},{2,66},{3,4},{4,68},{5,6},{6,70},{64,65},{65,1},{66,6... | collective-permute-start | bytes 196616 | tf_op jit(solution)/shard_map/ppermute | solution.py:427
  90.2 1.2 copy-start.3
  91.4 0.8 copy-start.5
  113.1 23.3 %collective-permute-start.14 = (f32[6,136,128]{2,1,0:T(8,128)S(1)}, f32[6,136,128]{2,1,0:T(8,128)S(1)}, u32[]{:S(2)}, u32[]{:S(2)}) collective-permute-start(f32[6,136,128]{2,1,0:T(8,128)S(1)} %get-tuple-element.50), channel_id=1, source_target_pairs={{0,8},{8,16},{16,24},{24,32},{32,40},{40,48},{48,56},{1,9},{9,17},... | collective-permute-start | bytes 1253384 | tf_op jit(solution)/shard_map/ppermute | solution.py:447
  114.4 31.8 %collective-permute-start.12 = (f32[6,136,128]{2,1,0:T(8,128)S(1)}, f32[6,136,128]{2,1,0:T(8,128)S(1)}, u32[]{:S(2)}, u32[]{:S(2)}) collective-permute-start(f32[6,136,128]{2,1,0:T(8,128)S(1)} %get-tuple-element.49), channel_id=1, source_target_pairs={{8,0},{16,8},{24,16},{32,24},{40,32},{48,40},{56,48},{9,1},{17,9},... | collective-permute-start | bytes 1253384 | tf_op jit(solution)/shard_map/ppermute | solution.py:447
  126.4 31.5 %collective-permute-start.16 = (f32[2,64,8,128]{3,2,1,0:T(8,128)S(1)}, f32[2,64,8,128]{3,2,1,0:T(8,128)S(1)}, u32[]{:S(2)}, u32[]{:S(2)}) collective-permute-start(f32[2,64,8,128]{3,2,1,0:T(8,128)S(1)} %iterate.8.refs_0_), channel_id=1, source_target_pairs={{0,64},{64,0},{1,65},{65,1},{2,66},{66,2},{3,67},{67,3},{4,68},{68... | collective-permute-start | bytes 1572872 | tf_op jit(solution)/shard_map/ppermute | solution.py:454
  136.3 20.9 %collective-permute-start.17 = (f32[2,64,8,128]{3,2,1,0:T(8,128)S(1)}, f32[2,64,8,128]{3,2,1,0:T(8,128)S(1)}, u32[]{:S(2)}, u32[]{:S(2)}) collective-permute-start(f32[2,64,8,128]{3,2,1,0:T(8,128)S(1)} %iterate.9.refs_0_), channel_id=1, source_target_pairs={{0,64},{64,0},{1,65},{65,1},{2,66},{66,2},{3,67},{67,3},{4,68},{68... | collective-permute-start | bytes 1572872 | tf_op jit(solution)/shard_map/ppermute | solution.py:454
  144.0 20.1 %collective-permute-start.15 = (f32[2,64,8,128]{3,2,1,0:T(8,128)S(1)}, f32[2,64,8,128]{3,2,1,0:T(8,128)S(1)}, u32[]{:S(2)}, u32[]{:S(2)}) collective-permute-start(f32[2,64,8,128]{3,2,1,0:T(8,128)S(1)} %iterate.7.refs_0_), channel_id=1, source_target_pairs={{0,64},{64,0},{1,65},{65,1},{2,66},{66,2},{3,67},{67,3},{4,68},{68... | collective-permute-start | bytes 1572872 | tf_op jit(solution)/shard_map/ppermute | solution.py:454
  153.8 18.7 %collective-permute-start.13 = (f32[2,64,8,128]{3,2,1,0:T(8,128)S(1)}, f32[2,64,8,128]{3,2,1,0:T(8,128)S(1)}, u32[]{:S(2)}, u32[]{:S(2)}) collective-permute-start(f32[2,64,8,128]{3,2,1,0:T(8,128)S(1)} %iterate.6.refs_0_), channel_id=1, source_target_pairs={{0,64},{64,0},{1,65},{65,1},{2,66},{66,2},{3,67},{67,3},{4,68},{68... | collective-permute-start | bytes 1572872 | tf_op jit(solution)/shard_map/ppermute | solution.py:454

commit v4 on v3

--- a/solution.py
+++ b/solution.py
@@ -20,6 +20,8 @@
 EXT_R = ROWS + 2 * PAD
 EXT_C = HALF + 2 * MARGIN
 MIB = 1024 * 1024
+UNROLL = 8
+UPDATE = 128
 TINY = 1e-30
 
 
@@ -70,46 +72,66 @@
     )(kz)
 
 
-def turn_kernel(where_ref, own_ref, other_ref, out_ref):
-    own = own_ref.reshape(Z * GROUP, CHUNK)
-    other = other_ref.reshape(Z * GROUP, CHUNK)
-    first = where_ref[1] == 0
-    for y in range(GROUP):
-        mine = own[pl.ds(y, Z, stride=GROUP), :]
-        theirs = other[pl.ds(y, Z, stride=GROUP), :]
-        pair = jnp.concatenate(
-            [jnp.where(first, mine, theirs), jnp.where(first, theirs, mine)], axis=0
+def turn_kernel(groups, where_ref, own_ref, other_ref, out_ref, west_ref, east_ref, own, other, sems):
+    half, first = where_ref[0], where_ref[1] == 0
+    blocks = [(i, j) for i in range(len(groups)) for j in range(2)]
+    copies = []
+    for n, (i, j) in enumerate(blocks):
+        at = pl.multiple_of(half * HALF + j * CHUNK, CHUNK)
+        mine = own_ref.at[0, :, pl.ds(groups[i] * GROUP, GROUP), pl.ds(at, CHUNK)]
+        theirs = other_ref.at[:, pl.ds(i * GROUP, GROUP), pl.ds(j * CHUNK, CHUNK)]
+        copies.append(
+            (
+                pltpu.make_async_copy(mine, own.at[n], sems.at[0, n]),
+                pltpu.make_async_copy(theirs, other.at[n], sems.at[1, n]),
+            )
         )
-        out_ref[y] = pair.T
-
-
-def turn(where, recorded, received, first_group, group_step):
-    count = received.shape[1] // GROUP
+    for pair in copies:
+        for c in pair:
+            c.start()
+    for n, (i, j) in enumerate(blocks):
+        for c in copies[n]:
+            c.wait()
+        flat = own.at[n].reshape(Z * GROUP, CHUNK)
+        flat_other = other.at[n].reshape(Z * GROUP, CHUNK)
+        for y in range(GROUP):
+            mine = flat[pl.ds(y, Z, stride=GROUP), :]
+            theirs = flat_other[pl.ds(y, Z, stride=GROUP), :]
+            pair = jnp.concatenate(
+                [jnp.where(first, mine, theirs), jnp.where(first, theirs, mine)], axis=0
+            ).T
+            row = i * GROUP + y
+            out_ref[row, pl.ds(j * CHUNK, CHUNK), :] = pair
+            if j == 0:
+                east_ref[row] = pair[:MARGIN]
+            else:
+                west_ref[row] = pair[CHUNK - MARGIN :]
+
+
+def turn(where, recorded, received, groups):
+    rows = len(groups) * GROUP
+    block = pltpu.VMEM((2 * len(groups), Z, GROUP, CHUNK), jnp.float32)
+    strip = jax.ShapeDtypeStruct((rows, MARGIN, LANES), jnp.float32)
     return pl.pallas_call(
-        turn_kernel,
-        out_shape=jax.ShapeDtypeStruct((count * GROUP, HALF, LANES), jnp.float32),
-        grid_spec=pltpu.PrefetchScalarGridSpec(
-            num_scalar_prefetch=1,
-            grid=(count, 2),
-            in_specs=[
-                pl.BlockSpec(
-                    (1, Z, GROUP, CHUNK),
-                    lambda i, j, w: (0, 0, first_group + group_step * i, 2 * w[0] + j),
-                ),
-                pl.BlockSpec((Z, GROUP, CHUNK), lambda i, j, w: (0, i, j)),
-            ],
-            out_specs=pl.BlockSpec((GROUP, CHUNK, LANES), lambda i, j, w: (i, j, 0)),
+        functools.partial(turn_kernel, groups),
+        out_shape=(jax.ShapeDtypeStruct((rows, HALF, LANES), jnp.float32), strip, strip),
+        in_specs=[
+            pl.BlockSpec(memory_space=pltpu.SMEM),
+            pl.BlockSpec(memory_space=pltpu.HBM),
+            pl.BlockSpec(memory_space=pl.ANY),
+        ],
+        out_specs=(pl.BlockSpec(memory_space=pltpu.VMEM),) * 3,
+        scratch_shapes=[block, block, pltpu.SemaphoreType.DMA((2, 2 * len(groups)))],
+        cost_estimate=pl.CostEstimate(
+            flops=0, bytes_accessed=len(groups) << 21, transcendentals=0
         ),
-        cost_estimate=pl.CostEstimate(
-            flops=0, bytes_accessed=count << 21, transcendentals=0
-        ),
-        compiler_params=params(8),
+        compiler_params=params(10),
         name="turn",
     )(where, recorded, received)
 
 
 SPANS = ((0, PAD),) + tuple((PAD + GROUP * g, GROUP) for g in range(4)) + ((EXT_R - PAD, PAD),)
-HOMES = ((0, 0), (1, 0), (2, 0), (0, GROUP))
+HOMES = (((1, 0), (2, 0), (3, 0)), ((4, 0), (5, 0), (7, 0)), ((4, 8), (6, 0), (7, 8)), ((1, 8), (2, 8), (3, 8)))
 
 
 def iterate_kernel(first, row0, n_out, present, *refs):
@@ -120,7 +142,7 @@
     fold = (EXT_C - 2 * SIDE) // 2
     pieces = iter(refs)
     taken = [next(pieces) if there else None for there in present]
-    recorded, field, refs = taken[:11], taken[11:], tuple(pieces)
+    recorded, field, refs = taken[:9], taken[9:], tuple(pieces)
     taps_ref, blur_ref, adj_ref = refs[:3]
     refs = refs[3:]
     if first:
@@ -129,7 +151,7 @@
     else:
         out_ref, refs = refs[0], refs[1:]
     r_buf, e_buf, xz_buf, xr_buf, pack, tmp, r_sem, e_sem = refs
-    north, south = recorded[0], recorded[10]
+    north, south = recorded[0], recorded[8]
     lower = lax.broadcasted_iota(jnp.int32, (width, LANES), 1) < Z
 
     def window(span, lo, hi):
@@ -153,13 +175,9 @@
                 )
             )
         else:
-            home, base = HOMES[k - 1]
-            west, mid, east = recorded[1 + 3 * home : 4 + 3 * home]
-            for src, lo, hi in (
-                (west, 0, MARGIN),
-                (mid, MARGIN, MARGIN + HALF),
-                (east, MARGIN + HALF, EXT_C),
-            ):
+            ranges = ((0, MARGIN), (MARGIN, MARGIN + HALF), (MARGIN + HALF, EXT_C))
+            for (home, base), (lo, hi) in zip(HOMES[k - 1], ranges):
+                src = recorded[home]
                 c, d = max(lo, shift), min(hi, shift + width)
                 pairs.append(
                     (
@@ -189,6 +207,20 @@
         for c in group:
             c.start()
 
+    def over_rows(start, count, steps, unroll):
+        def rows_from(at, many):
+            for step in steps:
+                for slot in range(many):
+                    step(slot, at + slot)
+
+        def body(i, carry):
+            rows_from(start + unroll * i, unroll)
+            return carry
+
+        lax.fori_loop(0, count // unroll, body, 0)
+        if count % unroll:
+            rows_from(start + count - count % unroll, count % unroll)
+
     kx = [taps_ref[t : t + 1, :] for t in range(7)]
     ky = [taps_ref[8 + t : 9 + t, :] for t in range(7)]
     col_blocks = blocks_of(width)
@@ -211,9 +243,8 @@
         split = jnp.where(lower, high, e - high).astype(jnp.bfloat16)
         both = jnp.dot(split, blur_ref[...], preferred_element_type=jnp.float32)
         tmp[slot, pl.ds(8, width), :] = both[:, :LANES] + both[:, LANES:]
-        cols_pass(slot, kx, xz_buf, row)
-
-    for slot in range(2):
+
+    for slot in range(UNROLL):
         tmp[slot, pl.ds(0, 8), :] = jnp.zeros((8, LANES), jnp.float32)
         tmp[slot, pl.ds(8 + width, 8), :] = jnp.zeros((8, LANES), jnp.float32)
 
@@ -225,18 +256,15 @@
             c.wait()
         base, count = got[0] - row0, got[1] - got[0]
 
-        def body(i, carry, k=k, base=base):
-            for slot in range(2):
-                row = base + 2 * i + slot
-                if not first and k in (0, 5):
-                    packed = pack[0 if k == 0 else 1, 2 * i + slot]
-                    turned = pltpu.roll(packed, Z, 1)
-                    e_buf[row, pl.ds(0, fold), :] = jnp.where(lower[:fold], packed, turned)
-                    e_buf[row, pl.ds(fold, fold), :] = jnp.where(lower[:fold], turned, packed)
-                blur_row(slot, row)
-            return carry
-
-        lax.fori_loop(0, count // 2, body, 0)
+        def halo_row(slot, row, k=k, base=base):
+            if not first and k in (0, 5):
+                packed = pack[0 if k == 0 else 1, row - base]
+                turned = pltpu.roll(packed, Z, 1)
+                e_buf[row, pl.ds(0, fold), :] = jnp.where(lower[:fold], packed, turned)
+                e_buf[row, pl.ds(fold, fold), :] = jnp.where(lower[:fold], turned, packed)
+            blur_row(slot, row)
+
+        over_rows(base, count, (halo_row, lambda slot, row: cols_pass(slot, kx, xz_buf, row)), UNROLL)
 
     if not first:
         for group in recorded_in:
@@ -249,44 +277,34 @@
             acc = acc + taps[t] * src_ref[row - 3 + t, pl.ds(at, size), :]
         return acc
 
-    def ratio_body(i, carry):
-        for slot in range(2):
-            row = 3 + 2 * i + slot
-            for at, size in col_blocks:
-                blurred = rows_pass(xz_buf, ky, row, at, size)
-                ratio = r_buf[row, pl.ds(at, size), :] / jnp.maximum(blurred, TINY)
-                tmp[slot, pl.ds(8 + at, size), :] = ratio
-            cols_pass(slot, kx[::-1], xr_buf, row)
-        return carry
-
-    lax.fori_loop(0, (n_in - 6) // 2, ratio_body, 0)
-
-    def update_row(row):
-        spread = []
-        for at, size in blocks_of(inner, 64):
-            spread.append(rows_pass(xr_buf, ky[::-1], row, SIDE + at, size))
-        spread = jnp.concatenate(spread, axis=0)
-        high = spread.astype(jnp.bfloat16)
-        low = (spread - high.astype(jnp.float32)).astype(jnp.bfloat16)
-        both = jnp.dot(
-            jnp.concatenate([high, low], axis=1), adj_ref[...], preferred_element_type=jnp.float32
-        )
-        factor = both + pltpu.roll(both, Z, 1)
-        return e_buf[row, pl.ds(SIDE, inner), :] * factor
-
-    def update_body(i, carry, base=0):
-        for k in range(2):
-            y = base + 2 * i + k
-            new = update_row(PAD + y)
+    def ratio_row(slot, row):
+        for at, size in col_blocks:
+            blurred = rows_pass(xz_buf, ky, row, at, size)
+            ratio = r_buf[row, pl.ds(at, size), :] / jnp.maximum(blurred, TINY)
+            tmp[slot, pl.ds(8 + at, size), :] = ratio
+
+    over_rows(3, n_in - 6, (ratio_row, lambda slot, row: cols_pass(slot, kx[::-1], xr_buf, row)), UNROLL)
+
+    def update_row(slot, y):
+        row = PAD + y
+        for at, size in blocks_of(inner, UPDATE):
+            spread = rows_pass(xr_buf, ky[::-1], row, SIDE + at, size)
+            high = spread.astype(jnp.bfloat16)
+            low = (spread - high.astype(jnp.float32)).astype(jnp.bfloat16)
+            both = jnp.dot(
+                jnp.concatenate([high, low], axis=1),
+                adj_ref[...],
+                preferred_element_type=jnp.float32,
+            )
+            factor = both + pltpu.roll(both, Z, 1)
+            new = e_buf[row, pl.ds(SIDE + at, size), :] * factor
             if first:
-                out_ref[y] = new
+                out_ref[y, pl.ds(at, size), :] = new
             else:
-                for j in range(2):
-                    flat = out_ref.at[j].reshape(Z * GROUP, CHUNK)
-                    flat[pl.ds(y, Z, stride=GROUP), :] = new[j * CHUNK : (j + 1) * CHUNK].T[:Z]
-        return carry
-
-    lax.fori_loop(0, n_out // 2, update_body, 0)
+                flat = out_ref.at[at // CHUNK].reshape(Z * GROUP, CHUNK)
+                flat[pl.ds(y, Z, stride=GROUP), :] = new.T[:Z]
+
+    over_rows(0, n_out, (update_row,), UNROLL)
     if first:
         for y in range(PAD):
             for ref, row in ((top_ref, y), (low_ref, ROWS - PAD + y)):
@@ -301,9 +319,9 @@
     fold = (EXT_C - 2 * SIDE) // 2
     pieces = list(recorded) + (list(field) if field is not None else [])
     if not first and row0 >= PAD:
-        pieces[0] = pieces[11] = None
+        pieces[0] = pieces[9] = None
     if not first and row0 + n_in <= EXT_R - PAD:
-        pieces[10] = pieces[13] = None
+        pieces[8] = pieces[11] = None
     present = tuple(piece is not None for piece in pieces)
     pieces = [piece for piece in pieces if piece is not None]
     if first:
@@ -327,14 +345,14 @@
             row,
             row,
             pltpu.VMEM((2, PAD, fold, LANES), jnp.float32),
-            pltpu.VMEM((2, width + 16, LANES), jnp.float32),
+            pltpu.VMEM((UNROLL, width + 16, LANES), jnp.float32),
             pltpu.SemaphoreType.DMA((6, 3)),
             pltpu.SemaphoreType.DMA((6,)),
         ],
         cost_estimate=pl.CostEstimate(
-            flops=vregs * 1024 * 70, bytes_accessed=vregs * 4096 * 3, transcendentals=0
+            flops=0, bytes_accessed=vregs * 4096 if first else 4096, transcendentals=0
         ),
-        compiler_params=params(36 if first else 16),
+        compiler_params=params(30 if first else 13),
         name="iterate",
     )(*pieces, taps, blur, adj)
 
@@ -387,7 +405,7 @@
     up = [(b, a) for a, b in down]
     half = lax.rem(lax.axis_index("tx") + lax.axis_index("view"), 2)
 
-    def other_rows(*starts):
+    def other_rows(views_data, *starts):
         at = (1 - half) * HALF
         return jnp.concatenate(
             [
@@ -397,11 +415,13 @@
             axis=1,
         )
 
-    border_in = lax.ppermute(other_rows((0, GROUP), (ROWS - GROUP, GROUP)), "view", swap)
     raw = jnp.concatenate([psf_axial[0], psf_rows[0], psf_cols[0]])
     raw_other = lax.ppermute(raw, "view", swap)
-    upper, raw_other = lax.optimization_barrier((other_rows((GROUP, GROUP)), raw_other))
-    upper_in = lax.ppermute(upper, "view", swap)
+    border = other_rows(views_data, (0, GROUP), (ROWS - GROUP, GROUP))
+    raw, border = lax.optimization_barrier((raw, border))
+    border_in = lax.ppermute(border, "view", swap)
+    later, border = lax.optimization_barrier((views_data, border))
+    upper_in = lax.ppermute(other_rows(later, (GROUP, GROUP)), "view", swap)
 
     def norm(taps):
         parts = (taps[:21], taps[21:28], taps[28:35])
@@ -423,34 +443,42 @@
     where = jnp.stack([half, view]).astype(jnp.int32)
     there = (1 - half).astype(jnp.int32)[None]
 
-    def widen(block):
-        west = lax.ppermute(block[:, HALF - MARGIN :], ("view", "tx"), right)
-        east = lax.ppermute(block[:, :MARGIN], ("view", "tx"), left)
-        return west, block, east
-
-    border = widen(turn(where, views_data, border_in, 0, 3))
-    lower, border = lax.optimization_barrier((other_rows((2 * GROUP, GROUP)), border))
-    lower_in = lax.ppermute(lower, "view", swap)
+    def sides(west, east):
+        return lax.ppermute(west, ("view", "tx"), right), lax.ppermute(east, ("view", "tx"), left)
+
+    middle, to_east, to_west = turn(where, views_data, border_in, (0, 3))
+    west, east = sides(to_east, to_west)
+    last, west, east = lax.optimization_barrier(
+        (other_rows(later, (2 * GROUP, GROUP)), west, east)
+    )
+    border = (west, middle, east)
+    lower_in = lax.ppermute(last, "view", swap)
 
     def edge(rows):
         return jnp.concatenate([part[rows] for part in border], axis=1)
 
     north = lax.ppermute(edge(slice(2 * GROUP - PAD, 2 * GROUP)), "ty", down)
     south = lax.ppermute(edge(slice(0, PAD)), "ty", up)
-    upper = widen(turn(where, views_data, upper_in, 1, 1))
-    lower = widen(turn(where, views_data, lower_in, 2, 1))
-    recorded = (north,) + border + upper + lower + (south,)
+    upper, upper_east, upper_west = turn(where, views_data, upper_in, (1,))
+    lower, lower_east, lower_west = turn(where, views_data, lower_in, (2,))
+    west, east = sides(
+        jnp.concatenate([upper_east, lower_east]), jnp.concatenate([upper_west, lower_west])
+    )
+    recorded = (north,) + border + (west, upper, lower, east, south)
 
     estimate, top, low = iterate(
         recorded, None, taps, blur, adj, first=True, row0=0, n_out=ROWS
     )
-    field = (lax.ppermute(low, "ty", down), estimate, lax.ppermute(top, "ty", up))
-    whole = None
-    theirs = []
-    for group in (1, 2, 0, 3):
-        block = iterate(
+    def piece(group, field):
+        return iterate(
             recorded, field, taps, blur, adj, first=False, row0=GROUP * group, n_out=GROUP
         )
+
+    field = (lax.ppermute(low, "ty", down), estimate, lax.ppermute(top, "ty", up))
+    theirs = []
+    whole = None
+    for group in (1, 2, 0, 3):
+        block = piece(group, field)
         theirs.append((group, lax.ppermute(block, "view", swap)))
         whole = place(where[:1], block, whole, group)
     for group, block in theirs:

time: 174 us -> 168 us (0.966)
  waiting for transfers between devices: 51.2 us -> 61.2 us
  Pallas kernels: 62 us -> 52.4 us
  starting transfers between devices: 39.4 us -> 31.6 us
    ppermute x9 -> x7, waiting for transfers between devices: 19.9 us -> 43.9 us  [the longest x1 23.7 us: per_device(): lower_in = lax.ppermute(last, 'view', swap)]
    ppermute x1, waiting for transfers between devices: 18.4 us -> 0.01 us  [per_device(): raw_other = lax.ppermute(raw, 'view', swap)]
    pallas_call x5, Pallas kernels: 51 us -> 40.9 us  [iterate(): pl.pallas_call(functools.partial(iterate_kernel, first, row0, n_out, pres...]
    ppermute x9 -> x7, starting transfers between devices: 23.5 us -> 13.9 us  [the longest x2 6.67 us: sides(): lax.ppermute(west, ('view', 'tx'), right)]
    ppermute x4, waiting for transfers between devices: 12.9 us -> 17.4 us  [per_device(): theirs.append((group, lax.ppermute(block, 'view', swap)))]
    unnamed x20 -> x18, local copies, waits for them, and re-layouts: 5.87 us -> 7.29 us
    squeeze x1 -> x2, local copies, waits for them, and re-layouts: 2.65 us -> 3.52 us  [other_rows(): lax.dynamic_slice(views_data, (0, 0, row, at), (1, Z, rows, HALF))[0]]
  transfers between devices with their start and end apart: 18 -> 16, of which waited for: 7 -> 7; matrix products, arithmetic and copies ran while one was open for 7% -> 8% of each run, Pallas kernels for 23% -> 21%
where the time goes in v4:
time: 168 us
  waiting for transfers between devices  61.2 us (36%)
  Pallas kernels  52.4 us (31%)
  starting transfers between devices  31.6 us (19%)
  other arithmetic  11.1 us (7%)
  local copies, waits for them, and re-layouts  11.1 us (7%)
    pallas_call x5, Pallas kernels, iterate(): pl.pallas_call(functools.partial(iterate_kernel, first, row0, n_out, pres...  40.9 us
    ppermute x1, waiting for transfers between devices, per_device(): lower_in = lax.ppermute(last, 'view', swap)  23.7 us
    ppermute x4, waiting for transfers between devices, per_device(): theirs.append((group, lax.ppermute(block, 'view', swap)))  17.4 us
    ppermute x1, waiting for transfers between devices, per_device(): border_in = lax.ppermute(border, 'view', swap)  15.7 us
    unnamed x18, local copies, waits for them, and re-layouts  7.29 us
    ppermute x2, starting transfers between devices, sides(): lax.ppermute(west, ('view', 'tx'), right)  6.67 us
    pallas_call x8, Pallas kernels, place(): pl.pallas_call(place_kernel, out_shape=jax.ShapeDtypeStruct((Z, ROWS, 2 *...  6.45 us
    ppermute x2, starting transfers between devices, sides(): lax.ppermute(east, ('view', 'tx'), left)  5.16 us
  transfers between devices with their start and end apart: 16, of which 7 were waited for; matrix products, arithmetic and copies ran while one was open for 8% of the time, Pallas kernels for 21%

profile of v4, /device:TPU:90, one launch (start us, length us, event | category | flops | bytes accessed | tf_op | source)
XLA Modules:
  0.0 167.7 jit_solution(15720057200624152921)
XLA Ops:
  0.8 1.6 collective-permute-start.9
  2.4 1.3 dynamic-slice_bitcast_fusion.3
  4.2 2.2 %dynamic-slice_bitcast_fusion = (f32[64,8,256]{2,1,0:T(8,128)}, f32[64,8,256]{2,1,0:T(8,128)}) fusion(f32[1,64,32,512]{3,2,1,0:T(8,128)} %own_ref.5, s32[]{:T(128)S(6)} %select_n.26), kind=kLoop, calls=%fused_computation.3 | loop fusion | bytes 2097156 | tf_op jit(solution)/shard_map/squeeze | solution.py:412
  6.5 1.6 collective-permute-start.3
  10.2 1.3 slice_divide_fusion.4
  13.0 1.3 slice_divide_fusion.1
  14.3 15.7 %collective-permute-done.other_ref = f32[64,16,256]{2,1,0:T(8,128)S(1)} collective-permute-done((f32[64,16,256]{2,1,0:T(8,128)S(1)}, f32[64,16,256]{2,1,0:T(8,128)S(1)}, u32[]{:S(2)}, u32[]{:S(2)}) %collective-permute-start) | collective-permute-done | bytes 1048608 | tf_op jit(solution)/shard_map/ppermute | solution.py:422
  29.9 2.2 %copy-done = f32[1,64,32,512]{3,2,1,0:T(8,128)S(1)} copy-done((f32[1,64,32,512]{3,2,1,0:T(8,128)S(1)}, f32[1,64,32,512]{3,2,1,0:T(8,128)}, u32[]{:S(2)}) %copy-start) | copy-done | bytes 4194328
  32.1 1.7 %turn.3 = (f32[16,256,128]{2,1,0:T(8,128)S(1)}, f32[16,16,128]{2,1,0:T(8,128)S(1)}, f32[16,16,128]{2,1,0:T(8,128)S(1)}) custom-call(s32[2]{0:T(128)S(1)} %pad_add_fusion.where_ref, f32[1,64,32,512]{3,2,1,0:T(8,128)S(1)} %copy-done, f32[64,16,256]{2,1,0:T(8,128)S(1)} %collective-permute-done.other_ref), custom_call_target="tpu_custom_call" | custom-call | bytes 4194304 | tf_op jit(solution)/shard_map/turn/pallas_call | solution.py:115
  33.9 2.6 %collective-permute-start.1 = (f32[16,16,128]{2,1,0:T(8,128)S(1)}, f32[16,16,128]{2,1,0:T(8,128)S(1)}, u32[]{:S(2)}, u32[]{:S(2)}) collective-permute-start(f32[16,16,128]{2,1,0:T(8,128)S(1)} %get-tuple-element.51), channel_id=1, source_target_pairs={{0,64},{1,2},{2,66},{3,4},{4,68},{5,6},{6,70},{64,65},{65,1},{66,6... | collective-permute-start | bytes 393224 | tf_op jit(solution)/shard_map/ppermute | solution.py:447
  36.5 3.3 %collective-permute-start.2 = (f32[16,16,128]{2,1,0:T(8,128)S(1)}, f32[16,16,128]{2,1,0:T(8,128)S(1)}, u32[]{:S(2)}, u32[]{:S(2)}) collective-permute-start(f32[16,16,128]{2,1,0:T(8,128)S(1)} %get-tuple-element.52), channel_id=1, source_target_pairs={{64,0},{2,1},{66,2},{4,3},{68,4},{6,5},{70,6},{65,64},{1,65},{67,6... | collective-permute-start | bytes 393224 | tf_op jit(solution)/shard_map/ppermute | solution.py:447
  40.4 2.9 %collective-permute-done.2.refs_3_.refs_2_ = f32[16,16,128]{2,1,0:T(8,128)S(1)} collective-permute-done((f32[16,16,128]{2,1,0:T(8,128)S(1)}, f32[16,16,128]{2,1,0:T(8,128)S(1)}, u32[]{:S(2)}, u32[]{:S(2)}) %collective-permute-start.2) | collective-permute-done | bytes 131104 | tf_op jit(solution)/shard_map/ppermute | solution.py:447
  44.3 3.6 %collective-permute-start.7 = (f32[6,288,128]{2,1,0:T(8,128)}, f32[6,288,128]{2,1,0:T(8,128)}, u32[]{:S(2)}, u32[]{:S(2)}) collective-permute-start(f32[6,288,128]{2,1,0:T(8,128)} %pad_maximum_fusion.1), channel_id=1, source_target_pairs={{8,0},{16,8},{24,16},{32,24},{40,32},{48,40},{56,48},{9,1},{17,9},... | collective-permute-start | bytes 2654216 | tf_op jit(solution)/shard_map/ppermute | solution.py:461
  48.9 1.3 collective-permute-start.8
  51.0 2.0 %turn.4 = (f32[8,256,128]{2,1,0:T(8,128)S(1)}, f32[8,16,128]{2,1,0:T(8,128)S(1)}, f32[8,16,128]{2,1,0:T(8,128)S(1)}) custom-call(s32[2]{0:T(128)S(1)} %pad_add_fusion.where_ref, f32[1,64,32,512]{3,2,1,0:T(8,128)S(1)} %copy-done.1, f32[64,8,256]{2,1,0:T(8,128)} %collective-permute-done.3.other_ref), custom_call_target="tpu_custom_call" | custom-call | bytes 2097152 | tf_op jit(solution)/shard_map/turn/pallas_call | solution.py:115
  53.0 23.7 %collective-permute-done.4.other_ref = f32[64,8,256]{2,1,0:T(8,128)S(1)} collective-permute-done((f32[64,8,256]{2,1,0:T(8,128)S(1)}, f32[64,8,256]{2,1,0:T(8,128)S(1)}, u32[]{:S(2)}, u32[]{:S(2)}) %collective-permute-start.4) | collective-permute-done | bytes 524320 | tf_op jit(solution)/shard_map/ppermute | solution.py:455
  76.7 1.1 turn.5
  79.5 1.9 %collective-permute-start.6 = (f32[16,16,128]{2,1,0:T(8,128)}, f32[16,16,128]{2,1,0:T(8,128)S(1)}, u32[]{:S(2)}, u32[]{:S(2)}) collective-permute-start(f32[16,16,128]{2,1,0:T(8,128)} %pad_maximum_fusion.4), channel_id=1, source_target_pairs={{64,0},{2,1},{66,2},{4,3},{68,4},{6,5},{70,6},{65,64},{1,65},{67,6... | collective-permute-start | bytes 393224 | tf_op jit(solution)/shard_map/ppermute | solution.py:447
  82.1 4.1 %collective-permute-start.5 = (f32[16,16,128]{2,1,0:T(8,128)}, f32[16,16,128]{2,1,0:T(8,128)}, u32[]{:S(2)}, u32[]{:S(2)}) collective-permute-start(f32[16,16,128]{2,1,0:T(8,128)} %pad_maximum_fusion.3), channel_id=1, source_target_pairs={{0,64},{1,2},{2,66},{3,4},{4,68},{5,6},{6,70},{64,65},{65,1},{66,6... | collective-permute-start | bytes 393224 | tf_op jit(solution)/shard_map/ppermute | solution.py:447
  87.8 1.0 collective-permute-done.5.refs_4_.refs_3_
  88.8 1.2 copy-done.3
  91.7 16.2 %iterate.5 = (f32[32,272,128]{2,1,0:T(8,128)S(1)}, f32[6,136,128]{2,1,0:T(8,128)S(1)}, f32[6,136,128]{2,1,0:T(8,128)S(1)}) custom-call(f32[6,288,128]{2,1,0:T(8,128)} %collective-permute-done.8.refs_0_, f32[16,16,128]{2,1,0:T(8,128)S(1)} %collective-permute-done.1.refs_1_.refs_0_, f32[16,256,128]{2,1,0:T(8,128)S(1)} %get-tuple-element.54.refs_2_.refs_1_, ...), custom_call_target="tpu_custom_call" | custom-call | bytes 6488064 | tf_op jit(solution)/shard_map/iterate/pallas_call | solution.py:336
  108.0 1.3 collective-permute-start.12
  109.3 4.8 %collective-permute-start.10 = (f32[6,136,128]{2,1,0:T(8,128)S(1)}, f32[6,136,128]{2,1,0:T(8,128)S(1)}, u32[]{:S(2)}, u32[]{:S(2)}) collective-permute-start(f32[6,136,128]{2,1,0:T(8,128)S(1)} %get-tuple-element.67), channel_id=1, source_target_pairs={{8,0},{16,8},{24,16},{32,24},{40,32},{48,40},{56,48},{9,1},{17,9},... | collective-permute-start | bytes 1253384 | tf_op jit(solution)/shard_map/ppermute | solution.py:477
  114.1 6.1 %iterate.9.refs_0_ = f32[2,64,8,128]{3,2,1,0:T(8,128)S(1)} custom-call(f32[16,16,128]{2,1,0:T(8,128)S(1)} %collective-permute-done.1.refs_1_.refs_0_, f32[16,256,128]{2,1,0:T(8,128)S(1)} %get-tuple-element.54.refs_2_.refs_1_, f32[16,16,128]{2,1,0:T(8,128)S(1)} %collective-permute-done.2.refs_3_.refs_2_, ...), custom_call_target="tpu_custom_call" | custom-call | bytes 4096 | tf_op jit(solution)/shard_map/iterate/pallas_call | solution.py:336
  120.2 2.5 %collective-permute-start.15 = (f32[2,64,8,128]{3,2,1,0:T(8,128)S(1)}, f32[2,64,8,128]{3,2,1,0:T(8,128)S(1)}, u32[]{:S(2)}, u32[]{:S(2)}) collective-permute-start(f32[2,64,8,128]{3,2,1,0:T(8,128)S(1)} %iterate.9.refs_0_), channel_id=1, source_target_pairs={{0,64},{64,0},{1,65},{65,1},{2,66},{66,2},{3,67},{67,3},{4,68},{68... | collective-permute-start | bytes 1572872 | tf_op jit(solution)/shard_map/ppermute | solution.py:482
  122.7 6.1 %iterate.8.refs_0_ = f32[2,64,8,128]{3,2,1,0:T(8,128)S(1)} custom-call(f32[16,16,128]{2,1,0:T(8,128)S(1)} %collective-permute-done.1.refs_1_.refs_0_, f32[16,256,128]{2,1,0:T(8,128)S(1)} %get-tuple-element.54.refs_2_.refs_1_, f32[16,16,128]{2,1,0:T(8,128)S(1)} %collective-permute-done.2.refs_3_.refs_2_, ...), custom_call_target="tpu_custom_call" | custom-call | bytes 4096 | tf_op jit(solution)/shard_map/iterate/pallas_call | solution.py:336
  129.3 6.2 %iterate.7.refs_0_ = f32[2,64,8,128]{3,2,1,0:T(8,128)S(1)} custom-call(f32[6,288,128]{2,1,0:T(8,128)} %collective-permute-done.8.refs_0_, f32[16,16,128]{2,1,0:T(8,128)S(1)} %collective-permute-done.1.refs_1_.refs_0_, f32[16,256,128]{2,1,0:T(8,128)S(1)} %get-tuple-element.54.refs_2_.refs_1_, f32[16,16,128]{2,1,0:T(8,128)S(1)} %collective-permute-done.2.refs_3_.refs_2_, ...), custom_call_target="tpu_custom_call" | custom-call | bytes 4096 | tf_op jit(solution)/shard_map/iterate/pallas_call | solution.py:336
  135.5 2.1 %collective-permute-start.13 = (f32[2,64,8,128]{3,2,1,0:T(8,128)S(1)}, f32[2,64,8,128]{3,2,1,0:T(8,128)S(1)}, u32[]{:S(2)}, u32[]{:S(2)}) collective-permute-start(f32[2,64,8,128]{3,2,1,0:T(8,128)S(1)} %iterate.7.refs_0_), channel_id=1, source_target_pairs={{0,64},{64,0},{1,65},{65,1},{2,66},{66,2},{3,67},{67,3},{4,68},{68... | collective-permute-start | bytes 1572872 | tf_op jit(solution)/shard_map/ppermute | solution.py:482
  137.6 6.2 %iterate.6.refs_0_ = f32[2,64,8,128]{3,2,1,0:T(8,128)S(1)} custom-call(f32[16,16,128]{2,1,0:T(8,128)S(1)} %collective-permute-done.1.refs_1_.refs_0_, f32[16,256,128]{2,1,0:T(8,128)S(1)} %get-tuple-element.54.refs_2_.refs_1_, f32[16,16,128]{2,1,0:T(8,128)S(1)} %collective-permute-done.2.refs_3_.refs_2_, ...), custom_call_target="tpu_custom_call" | custom-call | bytes 4096 | tf_op jit(solution)/shard_map/iterate/pallas_call | solution.py:336
  148.7 9.3 %collective-permute-done.13.refs_0_ = f32[2,64,8,128]{3,2,1,0:T(8,128)S(1)} collective-permute-done((f32[2,64,8,128]{3,2,1,0:T(8,128)S(1)}, f32[2,64,8,128]{3,2,1,0:T(8,128)S(1)}, u32[]{:S(2)}, u32[]{:S(2)}) %collective-permute-start.13) | collective-permute-done | bytes 524320 | tf_op jit(solution)/shard_map/ppermute | solution.py:482
  158.9 8.0 %collective-permute-done.11.refs_0_ = f32[2,64,8,128]{3,2,1,0:T(8,128)S(1)} collective-permute-done((f32[2,64,8,128]{3,2,1,0:T(8,128)S(1)}, f32[2,64,8,128]{3,2,1,0:T(8,128)S(1)}, u32[]{:S(2)}, u32[]{:S(2)}) %collective-permute-start.11) | collective-permute-done | bytes 524320 | tf_op jit(solution)/shard_map/ppermute | solution.py:482
  (61 shorter events, 20.9 us)
Async XLA Ops:
  0.8 10.9 %collective-permute-start.9 = (f32[35]{0:T(128)S(1)}, f32[35]{0:T(128)S(1)}, u32[]{:S(2)}, u32[]{:S(2)}) collective-permute-start(f32[35]{0:T(128)S(1)} %pad_maximum_fusion.7), channel_id=1, source_target_pairs={{0,64},{64,0},{1,65},{65,1},{2,66},{66,2},{3,67},{67,3},{4,68},{68... | collective-permute-start | bytes 428 | tf_op jit(solution)/shard_map/ppermute | solution.py:419
  3.8 26.2 %collective-permute-start = (f32[64,16,256]{2,1,0:T(8,128)S(1)}, f32[64,16,256]{2,1,0:T(8,128)S(1)}, u32[]{:S(2)}, u32[]{:S(2)}) collective-permute-start(f32[64,16,256]{2,1,0:T(8,128)S(1)} %pad_maximum_fusion), channel_id=1, source_target_pairs={{0,64},{64,0},{1,65},{65,1},{2,66},{66,2},{3,67},{67,3},{4,68},{68... | collective-permute-start | bytes 3145736 | tf_op jit(solution)/shard_map/ppermute | solution.py:422
  6.5 44.5 %collective-permute-start.3 = (f32[64,8,256]{2,1,0:T(8,128)}, f32[64,8,256]{2,1,0:T(8,128)}, u32[]{:S(2)}, u32[]{:S(2)}) collective-permute-start(f32[64,8,256]{2,1,0:T(8,128)} %get-tuple-element.73), channel_id=1, source_target_pairs={{0,64},{64,0},{1,65},{65,1},{2,66},{66,2},{3,67},{67,3},{4,68},{68... | collective-permute-start | bytes 1572872 | tf_op jit(solution)/shard_map/ppermute | solution.py:424
  29.9 2.2 %copy-start = (f32[1,64,32,512]{3,2,1,0:T(8,128)S(1)}, f32[1,64,32,512]{3,2,1,0:T(8,128)}, u32[]{:S(2)}) copy-start(f32[1,64,32,512]{3,2,1,0:T(8,128)} %own_ref.5) | copy-start | bytes 12582916
  32.1 11.2 %copy-start.8 = (f32[64,8,256]{2,1,0:T(8,128)S(1)}, f32[64,8,256]{2,1,0:T(8,128)}, u32[]{:S(2)}) copy-start(f32[64,8,256]{2,1,0:T(8,128)} %get-tuple-element.57) | copy-start | bytes 1572868
  33.9 17.2 %copy-start.1 = (f32[1,64,32,512]{3,2,1,0:T(8,128)S(1)}, f32[1,64,32,512]{3,2,1,0:T(8,128)}, u32[]{:S(2)}) copy-start(f32[1,64,32,512]{3,2,1,0:T(8,128)} %own_ref.5) | copy-start | bytes 12582916
  33.9 6.5 %collective-permute-start.1 = (f32[16,16,128]{2,1,0:T(8,128)S(1)}, f32[16,16,128]{2,1,0:T(8,128)S(1)}, u32[]{:S(2)}, u32[]{:S(2)}) collective-permute-start(f32[16,16,128]{2,1,0:T(8,128)S(1)} %get-tuple-element.51), channel_id=1, source_target_pairs={{0,64},{1,2},{2,66},{3,4},{4,68},{5,6},{6,70},{64,65},{65,1},{66,6... | collective-permute-start | bytes 393224 | tf_op jit(solution)/shard_map/ppermute | solution.py:447
  36.5 6.9 %collective-permute-start.2 = (f32[16,16,128]{2,1,0:T(8,128)S(1)}, f32[16,16,128]{2,1,0:T(8,128)S(1)}, u32[]{:S(2)}, u32[]{:S(2)}) collective-permute-start(f32[16,16,128]{2,1,0:T(8,128)S(1)} %get-tuple-element.52), channel_id=1, source_target_pairs={{64,0},{2,1},{66,2},{4,3},{68,4},{6,5},{70,6},{65,64},{1,65},{67,6... | collective-permute-start | bytes 393224 | tf_op jit(solution)/shard_map/ppermute | solution.py:447
  43.3 33.4 %collective-permute-start.4 = (f32[64,8,256]{2,1,0:T(8,128)S(1)}, f32[64,8,256]{2,1,0:T(8,128)S(1)}, u32[]{:S(2)}, u32[]{:S(2)}) collective-permute-start(f32[64,8,256]{2,1,0:T(8,128)S(1)} %copy-done.8), channel_id=1, source_target_pairs={{0,64},{64,0},{1,65},{65,1},{2,66},{66,2},{3,67},{67,3},{4,68},{68... | collective-permute-start | bytes 1572872 | tf_op jit(solution)/shard_map/ppermute | solution.py:455
  44.3 44.5 %collective-permute-start.7 = (f32[6,288,128]{2,1,0:T(8,128)}, f32[6,288,128]{2,1,0:T(8,128)}, u32[]{:S(2)}, u32[]{:S(2)}) collective-permute-start(f32[6,288,128]{2,1,0:T(8,128)} %pad_maximum_fusion.1), channel_id=1, source_target_pairs={{8,0},{16,8},{24,16},{32,24},{40,32},{48,40},{56,48},{9,1},{17,9},... | collective-permute-start | bytes 2654216 | tf_op jit(solution)/shard_map/ppermute | solution.py:461
  48.9 40.0 %collective-permute-start.8 = (f32[6,288,128]{2,1,0:T(8,128)}, f32[6,288,128]{2,1,0:T(8,128)}, u32[]{:S(2)}, u32[]{:S(2)}) collective-permute-start(f32[6,288,128]{2,1,0:T(8,128)} %pad_maximum_fusion.2), channel_id=1, source_target_pairs={{0,8},{8,16},{16,24},{24,32},{32,40},{40,48},{48,56},{1,9},{9,17},... | collective-permute-start | bytes 2654216 | tf_op jit(solution)/shard_map/ppermute | solution.py:460
  77.9 1.0 copy-start.2
  79.5 8.3 %collective-permute-start.6 = (f32[16,16,128]{2,1,0:T(8,128)}, f32[16,16,128]{2,1,0:T(8,128)S(1)}, u32[]{:S(2)}, u32[]{:S(2)}) collective-permute-start(f32[16,16,128]{2,1,0:T(8,128)} %pad_maximum_fusion.4), channel_id=1, source_target_pairs={{64,0},{2,1},{66,2},{4,3},{68,4},{6,5},{70,6},{65,64},{1,65},{67,6... | collective-permute-start | bytes 393224 | tf_op jit(solution)/shard_map/ppermute | solution.py:447
  82.1 6.7 %collective-permute-start.5 = (f32[16,16,128]{2,1,0:T(8,128)}, f32[16,16,128]{2,1,0:T(8,128)}, u32[]{:S(2)}, u32[]{:S(2)}) collective-permute-start(f32[16,16,128]{2,1,0:T(8,128)} %pad_maximum_fusion.3), channel_id=1, source_target_pairs={{0,64},{1,2},{2,66},{3,4},{4,68},{5,6},{6,70},{64,65},{65,1},{66,6... | collective-permute-start | bytes 393224 | tf_op jit(solution)/shard_map/ppermute | solution.py:447
  86.4 0.6 copy-start.4
  87.0 0.6 copy-start.6
  88.8 1.2 copy-start.3
  90.0 0.8 copy-start.5
  90.9 0.8 copy-start.7
  108.0 21.3 %collective-permute-start.12 = (f32[6,136,128]{2,1,0:T(8,128)S(1)}, f32[6,136,128]{2,1,0:T(8,128)S(1)}, u32[]{:S(2)}, u32[]{:S(2)}) collective-permute-start(f32[6,136,128]{2,1,0:T(8,128)S(1)} %get-tuple-element.68), channel_id=1, source_target_pairs={{0,8},{8,16},{16,24},{24,32},{32,40},{40,48},{48,56},{1,9},{9,17},... | collective-permute-start | bytes 1253384 | tf_op jit(solution)/shard_map/ppermute | solution.py:477
  109.3 28.3 %collective-permute-start.10 = (f32[6,136,128]{2,1,0:T(8,128)S(1)}, f32[6,136,128]{2,1,0:T(8,128)S(1)}, u32[]{:S(2)}, u32[]{:S(2)}) collective-permute-start(f32[6,136,128]{2,1,0:T(8,128)S(1)} %get-tuple-element.67), channel_id=1, source_target_pairs={{8,0},{16,8},{24,16},{32,24},{40,32},{48,40},{56,48},{9,1},{17,9},... | collective-permute-start | bytes 1253384 | tf_op jit(solution)/shard_map/ppermute | solution.py:477
  120.2 26.9 %collective-permute-start.15 = (f32[2,64,8,128]{3,2,1,0:T(8,128)S(1)}, f32[2,64,8,128]{3,2,1,0:T(8,128)S(1)}, u32[]{:S(2)}, u32[]{:S(2)}) collective-permute-start(f32[2,64,8,128]{3,2,1,0:T(8,128)S(1)} %iterate.9.refs_0_), channel_id=1, source_target_pairs={{0,64},{64,0},{1,65},{65,1},{2,66},{66,2},{3,67},{67,3},{4,68},{68... | collective-permute-start | bytes 1572872 | tf_op jit(solution)/shard_map/ppermute | solution.py:482
  128.9 19.0 %collective-permute-start.14 = (f32[2,64,8,128]{3,2,1,0:T(8,128)S(1)}, f32[2,64,8,128]{3,2,1,0:T(8,128)S(1)}, u32[]{:S(2)}, u32[]{:S(2)}) collective-permute-start(f32[2,64,8,128]{3,2,1,0:T(8,128)S(1)} %iterate.8.refs_0_), channel_id=1, source_target_pairs={{0,64},{64,0},{1,65},{65,1},{2,66},{66,2},{3,67},{67,3},{4,68},{68... | collective-permute-start | bytes 1572872 | tf_op jit(solution)/shard_map/ppermute | solution.py:482
  135.5 22.6 %collective-permute-start.13 = (f32[2,64,8,128]{3,2,1,0:T(8,128)S(1)}, f32[2,64,8,128]{3,2,1,0:T(8,128)S(1)}, u32[]{:S(2)}, u32[]{:S(2)}) collective-permute-start(f32[2,64,8,128]{3,2,1,0:T(8,128)S(1)} %iterate.7.refs_0_), channel_id=1, source_target_pairs={{0,64},{64,0},{1,65},{65,1},{2,66},{66,2},{3,67},{67,3},{4,68},{68... | collective-permute-start | bytes 1572872 | tf_op jit(solution)/shard_map/ppermute | solution.py:482
  143.8 23.1 %collective-permute-start.11 = (f32[2,64,8,128]{3,2,1,0:T(8,128)S(1)}, f32[2,64,8,128]{3,2,1,0:T(8,128)S(1)}, u32[]{:S(2)}, u32[]{:S(2)}) collective-permute-start(f32[2,64,8,128]{3,2,1,0:T(8,128)S(1)} %iterate.6.refs_0_), channel_id=1, source_target_pairs={{0,64},{64,0},{1,65},{65,1},{2,66},{66,2},{3,67},{67,3},{4,68},{68... | collective-permute-start | bytes 1572872 | tf_op jit(solution)/shard_map/ppermute | solution.py:482
